TPU v7x, 512 devices: a whole 4x4x16 slice. The times are simulated.
512 devices in a mesh: gx: 32 (over y_lo, z), gy: 16 (over x, y_hi, core).
Axes of the slice: x: 4, y: 4 (y_hi: 2, y_lo: 2; y = y_hi * 2 + y_lo), z: 16, core: 2. Of those that a mesh axis runs over, the one named last changes fastest.
Arguments:
- exciting: float32 [1024, 2, 20, 1536], P(('gx', 'gy')), may hold values from -6 to 6
- incident: float32 [1024, 2, 20, 1536], P(('gx', 'gy')), may hold values from -6 to 6
- pillar_type: int32 [1024, 1536], P(('gx', 'gy')), may hold values from 0 to 15
- type_matrix: float32 [16, 2, 20, 20], replicated, may hold values from -1 to 1
- near_coupling: float32 [2, 24, 20], replicated, may hold values from -1.2 to 1.2
- screening: float32 [20], replicated, may hold values from 1e-05 to 4
- coupling_gain: float32 [2, 20], replicated, may hold values from -6 to 6
Outputs:
- updated: float32 [1024, 2, 20, 1536], P(('gx', 'gy'))
Inputs may be any that keep to these rules, and one draw needn't show every extreme that they name: `pillar_type`: each pillar's type is one of the 16 types.
All inputs are finite; a program needn't handle non-finite values.
Results may differ from a plain program's by a relative error of at most 0.000073.
Values sent between devices are 32-bit elements; how exact they have to be, the bound alone decides.
A program may use at most 64 MiB of HBM per device.

v0:
```python
import functools
import math

import jax
import jax.numpy as jnp
import ml_dtypes
import numpy as np
from jax import lax
from jax.experimental import pallas as pl
from jax.experimental.pallas import tpu as pltpu
from jax.sharding import PartitionSpec as P

F32 = jnp.float32
BF16 = jnp.bfloat16
OUTER = 12
LANES = 128
GROUP = 24
VMEM_LIMIT = 60 * 1024 * 1024


def tables(width_x, coef, parts, slots, used):
    sine = np.arange(LANES)
    angle = 2.0 * np.pi / width_x * (np.arange(OUTER)[:, None] * sine[None, :])
    twiddle = np.stack([np.cos(angle), -np.sin(angle)], axis=1).astype(np.float32)
    angle = 2.0 * np.pi / LANES * (sine[:, None] * sine[None, :] % LANES)
    cosine, sines = np.cos(angle), np.sin(angle)
    forward = np.block([[cosine, -sines], [sines, cosine]])
    backward = np.block([[cosine, sines], [-sines, cosine]])

    def split(matrix):
        high = matrix.astype(ml_dtypes.bfloat16)
        return np.stack([high, (matrix - high.astype(np.float64)).astype(ml_dtypes.bfloat16)])

    flat = np.arange(parts)[:, None] * used + np.arange(slots)[None, :]
    freq = (flat // coef % OUTER)[:, :, None] + OUTER * sine[None, None, :]
    angle = 2.0 * np.pi / width_x * freq
    phase = np.stack([np.cos(angle), np.sin(angle), 4.0 * np.sin(angle / 2.0) ** 2], axis=1)
    return twiddle, split(forward), split(backward), phase.astype(np.float32)


def scale(value, factor):
    real, imag = value
    wr, wi = factor
    wr = round(wr) if abs(wr - round(wr)) < 1e-12 else wr
    wi = round(wi) if abs(wi - round(wi)) < 1e-12 else wi
    if wi == 0:
        return value if wr == 1 else ((-real, -imag) if wr == -1 else (wr * real, wr * imag))
    if wr == 0:
        return (-imag, real) if wi == 1 else ((imag, -real) if wi == -1 else (-wi * imag, wi * real))
    return (wr * real - wi * imag, wr * imag + wi * real)


def plus(left, right):
    return (left[0] + right[0], left[1] + right[1])


def minus(left, right):
    return (left[0] - right[0], left[1] - right[1])


def root(number, length, sign):
    angle = sign * 2.0 * math.pi * (number % length) / length
    return (math.cos(angle), math.sin(angle))


def four_points(values, sign):
    even, odd = plus(values[0], values[2]), minus(values[0], values[2])
    other, turn = plus(values[1], values[3]), scale(minus(values[1], values[3]), (0.0, sign))
    return [plus(even, other), plus(odd, turn), minus(even, other), minus(odd, turn)]


def twelve_points(values, sign):
    inner = [four_points(values[start::3], sign) for start in range(3)]
    result = [None] * 12
    for k4 in range(4):
        first = inner[0][k4]
        second = scale(inner[1][k4], root(k4, 12, sign))
        third = scale(inner[2][k4], root(2 * k4, 12, sign))
        total = plus(second, third)
        result[k4] = plus(first, total)
        centre = (first[0] - 0.5 * total[0], first[1] - 0.5 * total[1])
        side = scale(minus(second, third), (0.0, sign * math.sqrt(3.0) / 2.0))
        result[k4 + 4] = plus(centre, side)
        result[k4 + 8] = minus(centre, side)
    return result


def dot32(rows, matrix_ref):
    high = rows.astype(BF16)
    low = (rows - high.astype(F32)).astype(BF16)
    dot = functools.partial(jnp.dot, preferred_element_type=F32)
    return dot(high, matrix_ref[0]) + (dot(low, matrix_ref[0]) + dot(high, matrix_ref[1]))


def pieces(ka, coef, used):
    start, found = 0, []
    while start < coef:
        part, slot = divmod(ka * coef + start, used)
        count = min(coef - start, used - slot)
        found.append((start, part, slot, count))
        start += count
    return found


def stage_forward(dims, exciting, kinds, types, twiddle, matrix, send, stacked, field, work):
    rows, coef, width_x, used, slots, type_count = dims
    lane = lax.broadcasted_iota(jnp.int32, types.shape, 1)
    value = types[...]
    high = value.astype(BF16).astype(F32)
    stacked[...] = jnp.where(lane < 4 * GROUP, high, value - high).astype(BF16)
    chunk = 2 * LANES

    def add_chunk(index, carry):
        row = index // (width_x // chunk)
        col = index % (width_x // chunk)
        span = pl.ds(pl.multiple_of(col * chunk, chunk), chunk)
        empty = jnp.zeros((GROUP - coef, chunk), F32)
        joined = jnp.concatenate(
            [exciting[row, 0, :, span], empty, exciting[row, 1, :, span], empty], axis=0
        )
        top = joined.astype(BF16)
        low = (joined - top.astype(F32)).astype(BF16)
        products = jnp.dot(
            stacked[...], jnp.concatenate([top, low, top], axis=0), preferred_element_type=F32
        )
        kind = kinds[pl.ds(row, 1), span]
        total = products[: 2 * GROUP]
        for number in range(1, type_count):
            part = products[2 * GROUP * number : 2 * GROUP * (number + 1)]
            total = jnp.where(kind == number, part, total)
        for half in range(2):
            for part in range(2):
                field[row, 2 * col + half, part] = total[
                    part * GROUP : (part + 1) * GROUP, half * LANES : (half + 1) * LANES
                ]
        return carry

    lax.fori_loop(0, rows * (width_x // chunk), add_chunk, 0)
    blank = jnp.zeros((1, LANES), F32)
    for row in range(rows):

        def butterfly(step, carry, row=row):
            sub = pl.ds(pl.multiple_of(step * 8, 8), 8)
            values = [(field[row, a, 0, sub], field[row, a, 1, sub]) for a in range(OUTER)]
            values = twelve_points(values, -1.0)
            for ka in range(OUTER):
                real, imag = values[ka]
                wr, wi = twiddle[ka, 0:1, :], twiddle[ka, 1:2, :]
                work[row, ka, sub, 0:LANES] = real * wr - imag * wi
                work[row, ka, sub, LANES : 2 * LANES] = real * wi + imag * wr
            return carry

        lax.fori_loop(0, GROUP // 8, butterfly, 0)
        turned = dot32(work[row].reshape(OUTER * GROUP, 2 * LANES), matrix)
        for ka in range(OUTER):
            for start, dest, slot, count in pieces(ka, coef, used):
                for part in range(2):
                    send[dest, row, part, slot : slot + count, :] = turned[
                        ka * GROUP + start : ka * GROUP + start + count,
                        part * LANES : (part + 1) * LANES,
                    ]
        for dest in range(send.shape[0]):
            for part in range(2):
                send[dest, row, part, used:slots, :] = blank


def column_picker(gy, dims):
    rows, coef, width_x, used, slots, type_count = dims
    flat = gy * used + lax.broadcasted_iota(jnp.int32, (slots, coef), 0)
    hit = flat % coef == lax.broadcasted_iota(jnp.int32, (slots, coef), 1)

    def pick(line):
        return jnp.sum(jnp.where(hit, line, 0.0), axis=1, keepdims=True)

    return pick


def decay(gy, dims, phase, screening):
    pick = column_picker(gy, dims)
    level = pick(screening[...])
    shift = level + phase[gy, 2]
    small, large = jnp.sqrt(shift), jnp.sqrt(shift + 4.0)
    loss = 2.0 * small / (small + large)
    return pick, level, small * large, loss


def repeated(loss, count):
    for _ in range(int(math.log2(count))):
        loss = loss * (2.0 - loss)
    return loss


def stage_sums(gy, dims, held, phase, screening, send):
    rows, coef, width_x, used, slots, type_count = dims
    ratio = 1.0 - decay(gy, dims, phase, screening)[3]
    parts = held.shape[0]
    zero = jnp.zeros((slots, LANES), F32)
    ahead, back = (zero, zero), (zero, zero)
    for step in range(parts * rows):
        place, row = divmod(step, rows)
        ahead = tuple(ratio * ahead[p] + held[place, row, p] for p in range(2))
        place, row = divmod(parts * rows - 1 - step, rows)
        back = tuple(ratio * back[p] + held[place, row, p] for p in range(2))
    for slot in range(slots):
        for part in range(2):
            send[2 * slot, part : part + 1, :] = ahead[part][slot : slot + 1]
            send[2 * slot + 1, part : part + 1, :] = back[part][slot : slot + 1]


def stage_scan(gx, gy, dims, got, phase, screening, send, store):
    parts = phase.shape[0]
    rows = dims[0]
    groups = got.shape[0]
    loss = repeated(decay(gy, dims, phase, screening)[3], parts * rows)
    store[...] = loss
    loss = store[pl.ds(gx // 2, 1), :]
    side = gx % 2
    ratio = 1.0 - loss
    whole = repeated(loss, groups)
    total = jnp.zeros((2, LANES), F32)
    for step in range(groups):
        total = ratio * total + got[step + side * (groups - 1 - 2 * step)]
    total = total / whole
    for step in range(groups):
        place = step + side * (groups - 1 - 2 * step)
        send[place] = total
        total = ratio * total + got[place]


def stage_solve(
    gy, dims, held, before, after, ends, phase, screening, gain, coupling, send, edge, near
):
    rows, coef, width_x, used, slots, type_count = dims
    parts = held.shape[0]
    length = parts * rows
    pick, level, width, loss = decay(gy, dims, phase, screening)
    ratio = 1.0 - loss
    amplitude = jnp.sqrt(4.0 * math.pi * level) / (width * width_x)
    gain_real = pick(gain[0:1, :]) * amplitude
    gain_imag = pick(gain[1:2, :]) * amplitude
    for slot in range(slots):
        for part in range(2):
            edge[0, part, slot : slot + 1, :] = ends[2 * slot, part : part + 1, :]
            edge[1, part, slot : slot + 1, :] = ends[2 * slot + 1, part : part + 1, :]
    c1, s1 = phase[gy, 0], phase[gy, 1]
    c2, s2 = c1 * c1 - s1 * s1, 2.0 * c1 * s1
    turns = {-2: (c2, -s2), -1: (c1, -s1), 1: (c1, s1), 2: (c2, s2)}
    number = 0
    for dy in range(-2, 3):
        real = imag = jnp.zeros((slots, LANES), F32)
        for dx in range(-2, 3):
            if dx == 0 and dy == 0:
                continue
            wr = pick(coupling[0, number : number + 1, :]) * (1.0 / width_x)
            wi = pick(coupling[1, number : number + 1, :]) * (1.0 / width_x)
            number += 1
            if dx == 0:
                real, imag = real + wr, imag + wi
            else:
                tr, ti = turns[dx]
                real, imag = real + (wr * tr - wi * ti), imag + (wr * ti + wi * tr)
        near[dy + 2, 0] = real
        near[dy + 2, 1] = imag

    def line(step, part):
        if step < 0:
            return before[(step + rows) % rows, part]
        if step >= length:
            return after[step - length, part]
        return held[step // rows, step % rows, part]

    ahead = (edge[0, 0], edge[0, 1])
    for step in range(length):
        ahead = tuple(ratio * ahead[p] + line(step, p) for p in range(2))
        for part in range(2):
            send[step // rows, step % rows, part] = ahead[part]
    back = (edge[1, 0], edge[1, 1])
    for step in range(length - 1, -1, -1):
        back = tuple(ratio * back[p] for p in range(2))
        both = tuple(send[step // rows, step % rows, p] + back[p] for p in range(2))
        back = tuple(back[p] + line(step, p) for p in range(2))
        real = gain_real * both[0] - gain_imag * both[1]
        imag = gain_real * both[1] + gain_imag * both[0]
        for dy in range(-2, 3):
            wr, wi = near[dy + 2, 0], near[dy + 2, 1]
            lr, li = line(step + dy, 0), line(step + dy, 1)
            real = real + (wr * lr - wi * li)
            imag = imag + (wr * li + wi * lr)
        send[step // rows, step % rows, 0] = real
        send[step // rows, step % rows, 1] = imag


def stage_backward(dims, got, incident, twiddle, matrix, out, work):
    rows, coef, width_x, used, slots, type_count = dims
    for row in range(rows):
        for ka in range(OUTER):
            for start, place, slot, count in pieces(ka, coef, used):
                for part in range(2):
                    work[row, ka, start : start + count, part * LANES : (part + 1) * LANES] = got[
                        place, row, part, slot : slot + count, :
                    ]
            work[row, ka, coef:GROUP, :] = jnp.zeros((GROUP - coef, 2 * LANES), F32)
        turned = dot32(work[row].reshape(OUTER * GROUP, 2 * LANES), matrix)
        work[row] = turned.reshape(OUTER, GROUP, 2 * LANES)
        for low in range(0, coef, 8):
            count = min(8, coef - low)
            values = []
            for ka in range(OUTER):
                real = work[row, ka, low : low + count, 0:LANES]
                imag = work[row, ka, low : low + count, LANES : 2 * LANES]
                wr, wi = twiddle[ka, 0:1, :], twiddle[ka, 1:2, :]
                values.append((real * wr + imag * wi, imag * wr - real * wi))
            values = twelve_points(values, 1.0)
            for a in range(OUTER):
                for part in range(2):
                    place = (row, part, slice(low, low + count), slice(a * LANES, (a + 1) * LANES))
                    out[place] = incident[place] + values[a][part]


def call(kernel, outs, scratch, *args, interpret=False):
    return pl.pallas_call(
        kernel,
        out_shape=jax.ShapeDtypeStruct(outs, F32),
        in_specs=[pl.BlockSpec(memory_space=pltpu.VMEM)] * len(args),
        out_specs=pl.BlockSpec(memory_space=pltpu.VMEM),
        scratch_shapes=scratch,
        compiler_params=pltpu.CompilerParams(vmem_limit_bytes=VMEM_LIMIT),
        interpret=interpret,
    )(*args)


def type_rows(type_matrix):
    wide = jnp.pad(type_matrix, ((0, 0), (0, 0), (0, GROUP - type_matrix.shape[2]), (0, GROUP - type_matrix.shape[3])))
    real, imag = wide[:, 0], wide[:, 1]
    top = jnp.concatenate([real, -imag] * 3, axis=2)
    low = jnp.concatenate([imag, real] * 3, axis=2)
    return jnp.concatenate([top, low], axis=1).reshape(-1, 6 * GROUP)


def body(exciting, incident, pillar_type, type_matrix, near_coupling, screening, coupling_gain):
    rows, _, coef, width_x = exciting.shape
    groups = lax.axis_size("gx")
    parts = lax.axis_size("gy")
    used = OUTER * coef // parts
    slots = groups // 2
    dims = (rows, coef, width_x, used, slots, type_matrix.shape[0])
    twiddle, forward, backward, phase = tables(width_x, coef, parts, slots, used)
    screening = screening.reshape(1, coef)
    big = (parts, rows, 2, slots, LANES)
    small = (groups, 2, LANES)

    def run_forward(e, k, t, tw, m, send, stacked, field, work):
        stage_forward(dims, e, k, t, tw, m, send, stacked, field, work)

    types = type_rows(type_matrix)
    work = pltpu.VMEM((rows, OUTER, GROUP, 2 * LANES), F32)
    spread = call(
        run_forward,
        big,
        [
            pltpu.VMEM(types.shape, BF16),
            pltpu.VMEM((rows, OUTER, 2, GROUP, LANES), F32),
            work,
        ],
        exciting,
        pillar_type,
        types,
        twiddle,
        forward,
    )
    held = lax.all_to_all(spread, "gy", split_axis=0, concat_axis=0, tiled=True)

    def run_sums(held, phase, s, send):
        stage_sums(lax.axis_index("gy"), dims, held, phase, s, send)

    sums = call(run_sums, small, [], held, phase, screening)
    got = lax.all_to_all(sums, "gx", split_axis=0, concat_axis=0, tiled=True)
    up = [(i, (i + 1) % groups) for i in range(groups)]
    down = [((i + 1) % groups, i) for i in range(groups)]
    before = lax.ppermute(held[parts - 1], "gx", up)
    after = lax.ppermute(held[0], "gx", down)

    def run_scan(got, phase, s, send, store):
        stage_scan(lax.axis_index("gx"), lax.axis_index("gy"), dims, got, phase, s, send, store)

    ends = call(run_scan, small, [pltpu.VMEM((slots, LANES), F32)], got, phase, screening)
    ends = lax.all_to_all(ends, "gx", split_axis=0, concat_axis=0, tiled=True)

    def run_solve(held, before, after, ends, phase, s, g, n, send, edge, near):
        stage_solve(
            lax.axis_index("gy"), dims, held, before, after, ends, phase, s, g, n, send, edge, near
        )

    solved = call(
        run_solve,
        big,
        [pltpu.VMEM((2, 2, slots, LANES), F32), pltpu.VMEM((5, 2, slots, LANES), F32)],
        held,
        before,
        after,
        ends,
        phase,
        screening,
        coupling_gain,
        near_coupling,
    )
    back = lax.all_to_all(solved, "gy", split_axis=0, concat_axis=0, tiled=True)

    def run_backward(b, i, tw, m, out, work):
        stage_backward(dims, b, i, tw, m, out, work)

    return call(run_backward, exciting.shape, [work], back, incident, twiddle, backward)


def solution(mesh):
    placed = (
        P(("gx", "gy"), None, None, None),
        P(("gx", "gy"), None, None, None),
        P(("gx", "gy"), None),
        P(),
        P(),
        P(),
        P(),
    )
    return jax.shard_map(
        body,
        mesh=mesh,
        in_specs=placed,
        out_specs=P(("gx", "gy"), None, None, None),
        check_vma=False,
    )
```

profile of v0, /device:TPU:1, one launch (start us, length us, event | category | flops | bytes accessed | tf_op | source)
XLA Modules:
  0.0 106.9 jit_solution(10809282174254240761)
XLA Ops:
  0.0 1.4 %pad_slice_fusion.1 = (f32[16,1,24,24]{3,1,2,0:T(1,128)S(1)}, f32[16,1,24,24]{3,1,2,0:T(1,128)S(1)}) fusion(f32[16,2,20,20]{3,1,2,0:T(2,128)} %param.14), kind=kLoop, calls=%fused_computation.2 | loop fusion | bytes 124928 | tf_op jit(solution)/shard_map/slice | solution.py:334
  1.8 0.3 concatenate.9
  2.2 0.7 copy-done.1
  2.9 0.9 copy.13.e
  3.8 1.0 pad_maximum_fusion
  4.8 6.4 %shard_map.109 = f32[16,2,2,16,128]{4,3,2,1,0:T(8,128)} custom-call(f32[2,2,20,1536]{3,2,1,0:T(8,128)} %copy.13.e, s32[2,1536]{1,0:T(2,128)} %k.1, f32[768,144]{1,0:T(8,128)} %bitcast.20, f32[12,2,128]{2,1,0:T(2,128)} %constant.11.clone.tw, bf16[2,256,256]{2,1,0:T(8,128)(2,1)} %constant.12.clone.m), custom_call_target="tpu_custom_call" | custom-call | tf_op jit(solution)/shard_map/pallas_call | solution.py:321
  11.2 22.2 %all_to_all.20.held = f32[16,2,2,16,128]{4,3,2,1,0:T(8,128)} all-to-all(f32[16,2,2,16,128]{4,3,2,1,0:T(8,128)} %shard_map.109), channel_id=1, replica_groups=mesh['gx'=32,'gy'=16] {'gy'}, dimensions={0} | all-to-all | bytes 1048576 | tf_op jit(solution)/shard_map/all_to_all | solution.py:371
  33.4 2.0 %shard_map.110 = f32[32,2,128]{2,1,0:T(2,128)} custom-call(f32[16,2,2,16,128]{4,3,2,1,0:T(8,128)} %all_to_all.20.held, f32[16,3,16,128]{3,2,1,0:T(8,128)} %constant.13.clone.phase, f32[1,20]{1,0:T(1,128)} %bitcast.21), custom_call_target="tpu_custom_call" | custom-call | tf_op jit(solution)/shard_map/pallas_call | solution.py:321
  35.3 25.5 %all_to_all.21.got = f32[32,2,128]{2,1,0:T(2,128)} all-to-all(f32[32,2,128]{2,1,0:T(2,128)} %shard_map.110), channel_id=1, replica_groups=mesh['gx'=32,'gy'=16] {'gx'}, dimensions={0} | all-to-all | bytes 65536 | tf_op jit(solution)/shard_map/all_to_all | solution.py:377
  60.9 1.9 %shard_map.111 = f32[32,2,128]{2,1,0:T(2,128)} custom-call(f32[32,2,128]{2,1,0:T(2,128)} %all_to_all.21.got, f32[16,3,16,128]{3,2,1,0:T(8,128)} %constant.13.clone.phase, f32[1,20]{1,0:T(1,128)} %bitcast.22), custom_call_target="tpu_custom_call" | custom-call | tf_op jit(solution)/shard_map/pallas_call | solution.py:321
  62.7 3.8 %all-to-all-start.2 = ((f32[32,2,128]{2,1,0:T(2,128)}), f32[32,2,128]{2,1,0:T(2,128)S(1)}, u32[]{:S(2)}, u32[]{:S(2)}) async-start(f32[32,2,128]{2,1,0:T(2,128)} %shard_map.111), calls=%async_computation.2 | async-start | bytes 65536 | tf_op jit(solution)/shard_map/all_to_all | solution.py:387
  66.6 0.8 slice_bitcast_fusion
  67.4 3.0 %collective-permute-start = (f32[2,2,16,128]{3,2,1,0:T(8,128)S(1)}, f32[2,2,16,128]{3,2,1,0:T(8,128)S(1)}, u32[]{:S(2)}, u32[]{:S(2)}) collective-permute-start(f32[2,2,16,128]{3,2,1,0:T(8,128)S(1)} %get-tuple-element.6), channel_id=1, source_target_pairs={{0,16},{16,32},{32,48},{48,64},{64,80},{80,96},{96,112},{112,128},... | collective-permute-start | bytes 98312 | tf_op jit(solution)/shard_map/ppermute | solution.py:380
  70.4 4.4 %collective-permute-start.1 = (f32[2,2,16,128]{3,2,1,0:T(8,128)S(1)}, f32[2,2,16,128]{3,2,1,0:T(8,128)S(1)}, u32[]{:S(2)}, u32[]{:S(2)}) collective-permute-start(f32[2,2,16,128]{3,2,1,0:T(8,128)S(1)} %get-tuple-element.5), channel_id=1, source_target_pairs={{16,0},{32,16},{48,32},{64,48},{80,64},{96,80},{112,96},{128,112},... | collective-permute-start | bytes 98312 | tf_op jit(solution)/shard_map/ppermute | solution.py:381
  74.8 0.7 copy.14.n
  75.8 3.3 %all-to-all-done.2.ends = f32[32,2,128]{2,1,0:T(2,128)S(1)} async-done(((f32[32,2,128]{2,1,0:T(2,128)}), f32[32,2,128]{2,1,0:T(2,128)S(1)}, u32[]{:S(2)}, u32[]{:S(2)}) %all-to-all-start.2) | async-done | bytes 32800 | tf_op jit(solution)/shard_map/all_to_all | solution.py:387
  79.1 0.6 copy-done.3
  79.7 2.7 %shard_map.112 = f32[16,2,2,16,128]{4,3,2,1,0:T(8,128)} custom-call(f32[16,2,2,16,128]{4,3,2,1,0:T(8,128)} %all_to_all.20.held, f32[2,2,16,128]{3,2,1,0:T(8,128)} %copy-done.4, f32[2,2,16,128]{3,2,1,0:T(8,128)} %copy-done.5, f32[32,2,128]{2,1,0:T(2,128)} %copy-done.3, f32[16,3,16,128]{3,2,1,0:T(8,128)} %constant.13.clone.phase, f32[1,20]{1,0:T(1,128)} %bitcast.23, ...), custom_call_target="tpu_custom_call" | custom-call | tf_op jit(solution)/shard_map/pallas_call | solution.py:321
  82.4 7.5 %all-to-all-start.3 = ((f32[16,2,2,16,128]{4,3,2,1,0:T(8,128)}), f32[16,2,2,16,128]{4,3,2,1,0:T(8,128)S(1)}, u32[]{:S(2)}, u32[]{:S(2)}) async-start(f32[16,2,2,16,128]{4,3,2,1,0:T(8,128)} %shard_map.112), calls=%async_computation.3 | async-start | bytes 1048576 | tf_op jit(solution)/shard_map/all_to_all | solution.py:407
  89.9 0.9 copy.15.i
  90.8 10.3 %all-to-all-done.3.b = f32[16,2,2,16,128]{4,3,2,1,0:T(8,128)S(1)} async-done(((f32[16,2,2,16,128]{4,3,2,1,0:T(8,128)}), f32[16,2,2,16,128]{4,3,2,1,0:T(8,128)S(1)}, u32[]{:S(2)}, u32[]{:S(2)}) %all-to-all-start.3) | async-done | bytes 524320 | tf_op jit(solution)/shard_map/all_to_all | solution.py:407
  101.1 0.8 copy-done
  101.9 2.7 %shard_map.113 = f32[2,2,20,1536]{3,2,1,0:T(8,128)} custom-call(f32[16,2,2,16,128]{4,3,2,1,0:T(8,128)} %copy-done, f32[2,2,20,1536]{3,2,1,0:T(8,128)} %copy.15.i, f32[12,2,128]{2,1,0:T(2,128)} %constant.11.clone.tw, bf16[2,256,256]{2,1,0:T(8,128)(2,1)} %constant.14.clone.m), custom_call_target="tpu_custom_call" | custom-call | tf_op jit(solution)/shard_map/pallas_call | solution.py:321
  104.6 2.2 %copy.16 = f32[2,2,20,1536]{3,1,2,0:T(2,128)} copy(f32[2,2,20,1536]{3,2,1,0:T(8,128)} %shard_map.113) | data formatting | bytes 983040 | tf_op jit(solution)/shard_map/pallas_call | solution.py:321
  (15 shorter events, 0.7 us)
Async XLA Ops:
  1.8 1.0 copy-start.1
  62.7 16.4 %all-to-all-start.2 = ((f32[32,2,128]{2,1,0:T(2,128)}), f32[32,2,128]{2,1,0:T(2,128)S(1)}, u32[]{:S(2)}, u32[]{:S(2)}) async-start(f32[32,2,128]{2,1,0:T(2,128)} %shard_map.111), calls=%async_computation.2 | async-start | bytes 65536 | tf_op jit(solution)/shard_map/all_to_all | solution.py:387
  66.6 8.2 %copy-start.6 = (f32[2,24,20]{1,0,2:T(2,128)S(1)}, f32[2,24,20]{1,0,2:T(2,128)}, u32[]{:S(2)}) copy-start(f32[2,24,20]{1,0,2:T(2,128)} %param.15) | copy-start | bytes 11524
  67.4 8.1 %collective-permute-start = (f32[2,2,16,128]{3,2,1,0:T(8,128)S(1)}, f32[2,2,16,128]{3,2,1,0:T(8,128)S(1)}, u32[]{:S(2)}, u32[]{:S(2)}) collective-permute-start(f32[2,2,16,128]{3,2,1,0:T(8,128)S(1)} %get-tuple-element.6), channel_id=1, source_target_pairs={{0,16},{16,32},{32,48},{48,64},{64,80},{80,96},{96,112},{112,128},... | collective-permute-start | bytes 98312 | tf_op jit(solution)/shard_map/ppermute | solution.py:380
  70.4 5.4 %collective-permute-start.1 = (f32[2,2,16,128]{3,2,1,0:T(8,128)S(1)}, f32[2,2,16,128]{3,2,1,0:T(8,128)S(1)}, u32[]{:S(2)}, u32[]{:S(2)}) collective-permute-start(f32[2,2,16,128]{3,2,1,0:T(8,128)S(1)} %get-tuple-element.5), channel_id=1, source_target_pairs={{16,0},{32,16},{48,32},{64,48},{80,64},{96,80},{112,96},{128,112},... | collective-permute-start | bytes 98312 | tf_op jit(solution)/shard_map/ppermute | solution.py:381
  75.5 3.6 %copy-start.4 = (f32[2,2,16,128]{3,2,1,0:T(8,128)}, f32[2,2,16,128]{3,2,1,0:T(8,128)S(1)}, u32[]{:S(2)}) copy-start(f32[2,2,16,128]{3,2,1,0:T(8,128)S(1)} %collective-permute-done.before) | copy-start | bytes 98308
  75.8 3.3 %copy-start.5 = (f32[2,2,16,128]{3,2,1,0:T(8,128)}, f32[2,2,16,128]{3,2,1,0:T(8,128)S(1)}, u32[]{:S(2)}) copy-start(f32[2,2,16,128]{3,2,1,0:T(8,128)S(1)} %collective-permute-done.1.after) | copy-start | bytes 98308
  79.1 0.6 copy-start.3
  82.4 7.5 %copy-start.2 = (f32[2,2,20,1536]{3,1,2,0:T(2,128)S(1)}, f32[2,2,20,1536]{3,1,2,0:T(2,128)}, u32[]{:S(2)}) copy-start(f32[2,2,20,1536]{3,1,2,0:T(2,128)} %param.12) | copy-start | bytes 1474564
  82.4 18.7 %all-to-all-start.3 = ((f32[16,2,2,16,128]{4,3,2,1,0:T(8,128)}), f32[16,2,2,16,128]{4,3,2,1,0:T(8,128)S(1)}, u32[]{:S(2)}, u32[]{:S(2)}) async-start(f32[16,2,2,16,128]{4,3,2,1,0:T(8,128)} %shard_map.112), calls=%async_computation.3 | async-start | bytes 1048576 | tf_op jit(solution)/shard_map/all_to_all | solution.py:407
  101.1 0.8 copy-start
where the time goes:
time: 108 us; the launch traced here: 107 us
  blocking collectives  47.7 us (44%)
  starting transfers between devices  18.7 us (17%)
  Pallas kernels  15.6 us (14%)
  waiting for transfers between devices  14 us (13%)
  local copies, waits for them, and re-layouts  9.78 us (9%)
    all_to_all x1, blocking collectives, body(): got = lax.all_to_all(sums, 'gx', split_axis=0, concat_axis=0, tiled=True)  25.5 us
    all_to_all x1, blocking collectives, body(): held = lax.all_to_all(spread, 'gy', split_axis=0, concat_axis=0, tiled=True)  22.2 us
    pallas_call x5, Pallas kernels, call(): pl.pallas_call(kernel, out_shape=jax.ShapeDtypeStruct(outs, F32), in_spec...  15.6 us
    all_to_all x1, waiting for transfers between devices, body(): back = lax.all_to_all(solved, 'gy', split_axis=0, concat_axis=0, tiled=True)  10.3 us
    all_to_all x1, starting transfers between devices, body(): back = lax.all_to_all(solved, 'gy', split_axis=0, concat_axis=0, tiled=True)  7.49 us
    unnamed x17, local copies, waits for them, and re-layouts  4.64 us
    ppermute x1, starting transfers between devices, body(): after = lax.ppermute(held[0], 'gx', down)  4.37 us
    all_to_all x1, starting transfers between devices, body(): ends = lax.all_to_all(ends, 'gx', split_axis=0, concat_axis=0, tiled=True)  3.83 us
  transfers between devices with their start and end apart: 4, of which 3 were waited for; matrix products, arithmetic and copies ran while one was open for 2% of the time, Pallas kernels for 0%

commit v1 on v0

v1 whole, which is shorter than its diff:
```python
import functools
import math

import jax
import jax.numpy as jnp
import ml_dtypes
import numpy as np
from jax import lax
from jax.experimental import pallas as pl
from jax.experimental.pallas import tpu as pltpu
from jax.sharding import PartitionSpec as P

F32 = jnp.float32
BF16 = jnp.bfloat16
OUTER = 12
LANES = 128
GROUP = 24
VMEM_LIMIT = 60 * 1024 * 1024


def tables(width_x, coef, parts, slots, used):
    sine = np.arange(LANES)
    angle = 2.0 * np.pi / width_x * (np.arange(OUTER)[:, None] * sine[None, :])
    twiddle = np.stack([np.cos(angle), -np.sin(angle)], axis=1).astype(np.float32)
    angle = 2.0 * np.pi / LANES * (sine[:, None] * sine[None, :] % LANES)
    cosine, sines = np.cos(angle), np.sin(angle)
    forward = np.block([[cosine, -sines], [sines, cosine]])
    backward = np.block([[cosine, sines], [-sines, cosine]])

    def split(matrix):
        high = matrix.astype(ml_dtypes.bfloat16)
        return np.stack([high, (matrix - high.astype(np.float64)).astype(ml_dtypes.bfloat16)])

    flat = np.arange(parts)[:, None] * used + np.arange(slots)[None, :]
    freq = (flat // coef % OUTER)[:, :, None] + OUTER * sine[None, None, :]
    angle = 2.0 * np.pi / width_x * freq
    phase = np.stack([np.cos(angle), np.sin(angle), 4.0 * np.sin(angle / 2.0) ** 2], axis=1)
    return twiddle, split(forward), split(backward), phase.astype(np.float32)


def scale(value, factor):
    real, imag = value
    wr, wi = factor
    wr = round(wr) if abs(wr - round(wr)) < 1e-12 else wr
    wi = round(wi) if abs(wi - round(wi)) < 1e-12 else wi
    if wi == 0:
        return value if wr == 1 else ((-real, -imag) if wr == -1 else (wr * real, wr * imag))
    if wr == 0:
        return (-imag, real) if wi == 1 else ((imag, -real) if wi == -1 else (-wi * imag, wi * real))
    return (wr * real - wi * imag, wr * imag + wi * real)


def plus(left, right):
    return (left[0] + right[0], left[1] + right[1])


def minus(left, right):
    return (left[0] - right[0], left[1] - right[1])


def root(number, length, sign):
    angle = sign * 2.0 * math.pi * (number % length) / length
    return (math.cos(angle), math.sin(angle))


def four_points(values, sign):
    even, odd = plus(values[0], values[2]), minus(values[0], values[2])
    other, turn = plus(values[1], values[3]), scale(minus(values[1], values[3]), (0.0, sign))
    return [plus(even, other), plus(odd, turn), minus(even, other), minus(odd, turn)]


def twelve_points(values, sign):
    inner = [four_points(values[start::3], sign) for start in range(3)]
    result = [None] * 12
    for k4 in range(4):
        first = inner[0][k4]
        second = scale(inner[1][k4], root(k4, 12, sign))
        third = scale(inner[2][k4], root(2 * k4, 12, sign))
        total = plus(second, third)
        result[k4] = plus(first, total)
        centre = (first[0] - 0.5 * total[0], first[1] - 0.5 * total[1])
        side = scale(minus(second, third), (0.0, sign * math.sqrt(3.0) / 2.0))
        result[k4 + 4] = plus(centre, side)
        result[k4 + 8] = minus(centre, side)
    return result


def dot32(rows, matrix_ref):
    high = rows.astype(BF16)
    low = (rows - high.astype(F32)).astype(BF16)
    dot = functools.partial(jnp.dot, preferred_element_type=F32)
    return dot(high, matrix_ref[0]) + (dot(low, matrix_ref[0]) + dot(high, matrix_ref[1]))


def pieces(ka, coef, used):
    start, found = 0, []
    while start < coef:
        part, slot = divmod(ka * coef + start, used)
        count = min(coef - start, used - slot)
        found.append((start, part, slot, count))
        start += count
    return found


def stack_types(type_matrix, spread, stacked, coef):
    spread[...] = jnp.zeros_like(spread)

    def place(number, carry):
        real, imag = type_matrix[number, 0], type_matrix[number, 1]
        for copy in range(3):
            low = 2 * GROUP * copy
            spread[number, 0:coef, low : low + coef] = real
            spread[number, 0:coef, low + GROUP : low + GROUP + coef] = -imag
            spread[number, GROUP : GROUP + coef, low : low + coef] = imag
            spread[number, GROUP : GROUP + coef, low + GROUP : low + GROUP + coef] = real
        return carry

    lax.fori_loop(0, spread.shape[0], place, 0)
    value = spread[...].reshape(stacked.shape)
    lane = lax.broadcasted_iota(jnp.int32, value.shape, 1)
    high = value.astype(BF16).astype(F32)
    stacked[...] = jnp.where(lane < 4 * GROUP, high, value - high).astype(BF16)


def forward_row(row, dims, exciting, kinds, twiddle, matrix, send, stacked, field, work):
    rows, coef, width_x, used, slots, type_count = dims
    chunk = 2 * LANES

    def add_chunk(col, carry):
        span = pl.ds(pl.multiple_of(col * chunk, chunk), chunk)
        empty = jnp.zeros((GROUP - coef, chunk), F32)
        joined = jnp.concatenate(
            [exciting[row, 0, :, span], empty, exciting[row, 1, :, span], empty], axis=0
        )
        top = joined.astype(BF16)
        low = (joined - top.astype(F32)).astype(BF16)
        products = jnp.dot(
            stacked[...], jnp.concatenate([top, low, top], axis=0), preferred_element_type=F32
        )
        kind = kinds[row : row + 1, span]
        total = products[: 2 * GROUP]
        for number in range(1, type_count):
            part = products[2 * GROUP * number : 2 * GROUP * (number + 1)]
            total = jnp.where(kind == number, part, total)
        for half in range(2):
            for part in range(2):
                field[2 * col + half, part] = total[
                    part * GROUP : (part + 1) * GROUP, half * LANES : (half + 1) * LANES
                ]
        return carry

    lax.fori_loop(0, width_x // chunk, add_chunk, 0)

    def butterfly(step, carry):
        sub = pl.ds(pl.multiple_of(step * 8, 8), 8)
        values = [(field[a, 0, sub], field[a, 1, sub]) for a in range(OUTER)]
        values = twelve_points(values, -1.0)
        for ka in range(OUTER):
            real, imag = values[ka]
            wr, wi = twiddle[ka, 0:1, :], twiddle[ka, 1:2, :]
            work[ka, sub, 0:LANES] = real * wr - imag * wi
            work[ka, sub, LANES : 2 * LANES] = real * wi + imag * wr
        return carry

    lax.fori_loop(0, GROUP // 8, butterfly, 0)
    turned = dot32(work[...].reshape(OUTER * GROUP, 2 * LANES), matrix)
    for ka in range(OUTER):
        for start, dest, slot, count in pieces(ka, coef, used):
            for part in range(2):
                send[dest, row, part, slot : slot + count, :] = turned[
                    ka * GROUP + start : ka * GROUP + start + count,
                    part * LANES : (part + 1) * LANES,
                ]
    blank = jnp.zeros((slots - used, LANES), F32)
    for dest in range(send.shape[0]):
        for part in range(2):
            send[dest, row, part, used:slots, :] = blank


def column_picker(gy, dims):
    rows, coef, width_x, used, slots, type_count = dims
    flat = gy * used + lax.broadcasted_iota(jnp.int32, (slots, coef), 0)
    hit = flat % coef == lax.broadcasted_iota(jnp.int32, (slots, coef), 1)

    def pick(line):
        return jnp.sum(jnp.where(hit, line, 0.0), axis=1, keepdims=True)

    return pick


def decay(gy, dims, phase, screening):
    pick = column_picker(gy, dims)
    level = pick(screening[...])
    shift = level + phase[gy, 2]
    small, large = jnp.sqrt(shift), jnp.sqrt(shift + 4.0)
    loss = 2.0 * small / (small + large)
    return pick, level, small * large, loss


def repeated(loss, count):
    for _ in range(int(math.log2(count))):
        loss = loss * (2.0 - loss)
    return loss


def stage_backward(dims, got, incident, twiddle, matrix, out, work):
    rows, coef, width_x, used, slots, type_count = dims
    for row in range(rows):
        for ka in range(OUTER):
            for start, place, slot, count in pieces(ka, coef, used):
                for part in range(2):
                    work[ka, start : start + count, part * LANES : (part + 1) * LANES] = got[
                        place, row, part, slot : slot + count, :
                    ]
            work[ka, coef:GROUP, :] = jnp.zeros((GROUP - coef, 2 * LANES), F32)
        turned = dot32(work[...].reshape(OUTER * GROUP, 2 * LANES), matrix)
        work[...] = turned.reshape(OUTER, GROUP, 2 * LANES)
        for low in range(0, coef, 8):
            count = min(8, coef - low)
            values = []
            for ka in range(OUTER):
                real = work[ka, low : low + count, 0:LANES]
                imag = work[ka, low : low + count, LANES : 2 * LANES]
                wr, wi = twiddle[ka, 0:1, :], twiddle[ka, 1:2, :]
                values.append((real * wr + imag * wi, imag * wr - real * wi))
            values = twelve_points(values, 1.0)
            for a in range(OUTER):
                for part in range(2):
                    place = (row, part, slice(low, low + count), slice(a * LANES, (a + 1) * LANES))
                    out[place] = incident[place] + values[a][part]


def fused(
    dims,
    groups,
    parts,
    exciting,
    incident,
    kinds,
    type_matrix,
    coupling,
    screening,
    gain,
    twiddle,
    forward,
    inverse,
    phase,
    out,
    spread,
    stacked,
    field,
    work,
    send,
    held,
    sums,
    got,
    reply,
    ends,
    edge,
    near,
    level,
    ahead_all,
    back_all,
    solved,
    back,
    wide_send,
    wide_recv,
    small_send,
    small_recv,
    reply_send,
    reply_recv,
    halo_send,
    halo_recv,
    last_send,
    last_recv,
):
    rows, coef, width_x, used, slots, type_count = dims
    gx, gy = lax.axis_index("gx"), lax.axis_index("gy")
    length = parts * rows

    def near_peer(step):
        return lax.rem(gy + step, parts)

    def far_peer(step):
        return lax.rem(gx + step, groups)

    def remote(source, target, first, second, device):
        return pltpu.make_async_remote_copy(
            src_ref=source,
            dst_ref=target,
            send_sem=first,
            recv_sem=second,
            device_id=device,
            device_id_type=pl.DeviceIdType.MESH,
        )

    def each(low, high, act):
        def run(step, carry):
            act(step)
            return carry

        lax.fori_loop(low, high, run, 0)

    barrier = pltpu.get_barrier_semaphore()

    def greet(device):
        pl.semaphore_signal(barrier, inc=1, device_id=device, device_id_type=pl.DeviceIdType.MESH)

    each(1, parts, lambda step: greet((gx, near_peer(step))))
    each(1, groups, lambda step: greet((far_peer(step), gy)))

    def wide(row, step):
        peer = near_peer(step)
        return remote(
            send.at[peer, row],
            held.at[1 + gy, row],
            wide_send.at[row, step],
            wide_recv.at[row, step],
            (gx, peer),
        )

    def small(step):
        peer = far_peer(step)
        return remote(
            sums.at[peer], got.at[gx], small_send.at[step], small_recv.at[step], (peer, gy)
        )

    def answer(step):
        peer = far_peer(step)
        return remote(
            reply.at[peer], ends.at[gx], reply_send.at[step], reply_recv.at[step], (peer, gy)
        )

    def last(step):
        peer = near_peer(step)
        return remote(
            solved.at[peer], back.at[gy], last_send.at[step], last_recv.at[step], (gx, peer)
        )

    up = remote(
        held.at[parts], held.at[0], halo_send.at[0], halo_recv.at[0], (far_peer(1), gy)
    )
    down = remote(
        held.at[1],
        held.at[parts + 1],
        halo_send.at[1],
        halo_recv.at[1],
        (far_peer(groups - 1), gy),
    )

    stack_types(type_matrix, spread, stacked, coef)
    for row in range(rows):
        forward_row(row, dims, exciting, kinds, twiddle, forward, send, stacked, field, work)
        if row == 0:
            pl.semaphore_wait(barrier, parts + groups - 2)
        each(1, parts, lambda step, row=row: wide(row, step).start())
        held[1 + gy, row] = send[gy, row]

    pick, screen, width, loss = decay(gy, dims, phase, screening)
    ratio = 1.0 - loss
    amplitude = jnp.sqrt(4.0 * math.pi * screen) / (width * width_x)
    level[0] = pick(gain[0:1, :]) * amplitude
    level[1] = pick(gain[1:2, :]) * amplitude
    level[2] = repeated(loss, length)
    level[3] = ratio
    c1, s1 = phase[gy, 0], phase[gy, 1]
    c2, s2 = c1 * c1 - s1 * s1, 2.0 * c1 * s1
    turns = {-2: (c2, -s2), -1: (c1, -s1), 1: (c1, s1), 2: (c2, s2)}
    number = 0
    for dy in range(-2, 3):
        real = imag = jnp.zeros((slots, LANES), F32)
        for dx in range(-2, 3):
            if dx == 0 and dy == 0:
                continue
            wr = pick(coupling[0, number : number + 1, :]) * (1.0 / width_x)
            wi = pick(coupling[1, number : number + 1, :]) * (1.0 / width_x)
            number += 1
            if dx == 0:
                real, imag = real + wr, imag + wi
            else:
                tr, ti = turns[dx]
                real, imag = real + (wr * tr - wi * ti), imag + (wr * ti + wi * tr)
        near[dy + 2, 0] = real
        near[dy + 2, 1] = imag

    for row in range(rows):
        each(1, parts, lambda step, row=row: wide(row, step).wait_recv())
    up.start()
    down.start()
    ratio = level[3]
    zero = jnp.zeros((slots, LANES), F32)
    ahead, behind = (zero, zero), (zero, zero)
    for step in range(length):
        place, row = divmod(step, rows)
        ahead = tuple(ratio * ahead[p] + held[1 + place, row, p] for p in range(2))
        place, row = divmod(length - 1 - step, rows)
        behind = tuple(ratio * behind[p] + held[1 + place, row, p] for p in range(2))
    for slot in range(slots):
        for part in range(2):
            sums[2 * slot, part : part + 1, :] = ahead[part][slot : slot + 1]
            sums[2 * slot + 1, part : part + 1, :] = behind[part][slot : slot + 1]
    each(1, groups, lambda step: small(step).start())
    got[gx] = sums[gx]

    loss = level[2, pl.ds(gx // 2, 1), :]
    side = gx % 2
    ratio = 1.0 - loss
    whole = repeated(loss, groups)
    each(1, groups, lambda step: small(step).wait_recv())
    total = jnp.zeros((2, LANES), F32)
    for step in range(groups):
        total = ratio * total + got[step + side * (groups - 1 - 2 * step)]
    total = total / whole
    for step in range(groups):
        place = step + side * (groups - 1 - 2 * step)
        reply[place] = total
        total = ratio * total + got[place]
    each(1, groups, lambda step: answer(step).start())
    ends[gx] = reply[gx]
    each(1, groups, lambda step: answer(step).wait_recv())
    up.wait_recv()
    down.wait_recv()

    for slot in range(slots):
        for part in range(2):
            edge[0, part, slot : slot + 1, :] = ends[2 * slot, part : part + 1, :]
            edge[1, part, slot : slot + 1, :] = ends[2 * slot + 1, part : part + 1, :]
    ratio = level[3]
    ahead, behind = (edge[0, 0], edge[0, 1]), (edge[1, 0], edge[1, 1])
    for step in range(length):
        place, row = divmod(step, rows)
        ahead = tuple(ratio * ahead[p] + held[1 + place, row, p] for p in range(2))
        for p in range(2):
            ahead_all[place, row, p] = ahead[p]
        place, row = divmod(length - 1 - step, rows)
        behind = tuple(ratio * behind[p] for p in range(2))
        for p in range(2):
            back_all[place, row, p] = behind[p]
        behind = tuple(behind[p] + held[1 + place, row, p] for p in range(2))

    def combine(place, target):
        gain_real, gain_imag = level[0], level[1]
        for row in range(rows):
            both = tuple(ahead_all[place, row, p] + back_all[place, row, p] for p in range(2))
            real = gain_real * both[0] - gain_imag * both[1]
            imag = gain_real * both[1] + gain_imag * both[0]
            for dy in range(-2, 3):
                jump, other = divmod(row + dy, rows)
                wr, wi = near[dy + 2, 0], near[dy + 2, 1]
                lr = held[1 + place + jump, other, 0]
                li = held[1 + place + jump, other, 1]
                real = real + (wr * lr - wi * li)
                imag = imag + (wr * li + wi * lr)
            target[place, row, 0] = real
            target[place, row, 1] = imag

    def solve(step):
        combine(near_peer(step), solved)
        last(step).start()

    each(1, parts, solve)
    combine(gy, back)
    each(1, parts, lambda step: last(step).wait_recv())
    stage_backward(dims, back, incident, twiddle, inverse, out, work)

    for row in range(rows):
        each(1, parts, lambda step, row=row: wide(row, step).wait_send())
    each(1, groups, lambda step: small(step).wait_send())
    each(1, groups, lambda step: answer(step).wait_send())
    up.wait_send()
    down.wait_send()
    each(1, parts, lambda step: last(step).wait_send())


def body(exciting, incident, pillar_type, type_matrix, near_coupling, screening, coupling_gain):
    rows, _, coef, width_x = exciting.shape
    groups = lax.axis_size("gx")
    parts = lax.axis_size("gy")
    used = OUTER * coef // parts
    slots = groups // 2
    dims = (rows, coef, width_x, used, slots, type_matrix.shape[0])
    twiddle, forward, inverse, phase = tables(width_x, coef, parts, slots, used)
    args = (
        exciting,
        incident,
        pillar_type,
        type_matrix,
        near_coupling,
        screening.reshape(1, coef),
        coupling_gain,
        twiddle,
        forward,
        inverse,
        phase,
    )
    count = type_matrix.shape[0]
    big = pltpu.VMEM((parts, rows, 2, slots, LANES), F32)
    small = pltpu.VMEM((groups, 2, LANES), F32)
    dma = pltpu.SemaphoreType.DMA
    return pl.pallas_call(
        functools.partial(fused, dims, groups, parts),
        out_shape=jax.ShapeDtypeStruct(exciting.shape, F32),
        in_specs=[pl.BlockSpec(memory_space=pltpu.VMEM)] * len(args),
        out_specs=pl.BlockSpec(memory_space=pltpu.VMEM),
        scratch_shapes=[
            pltpu.VMEM((count, 2 * GROUP, 6 * GROUP), F32),
            pltpu.VMEM((count * 2 * GROUP, 6 * GROUP), BF16),
            pltpu.VMEM((OUTER, 2, GROUP, LANES), F32),
            pltpu.VMEM((OUTER, GROUP, 2 * LANES), F32),
            big,
            pltpu.VMEM((parts + 2, rows, 2, slots, LANES), F32),
            small,
            small,
            small,
            small,
            pltpu.VMEM((2, 2, slots, LANES), F32),
            pltpu.VMEM((5, 2, slots, LANES), F32),
            pltpu.VMEM((4, slots, LANES), F32),
            big,
            big,
            big,
            big,
            dma((rows, parts)),
            dma((rows, parts)),
            dma((groups,)),
            dma((groups,)),
            dma((groups,)),
            dma((groups,)),
            dma((2,)),
            dma((2,)),
            dma((parts,)),
            dma((parts,)),
        ],
        compiler_params=pltpu.CompilerParams(
            vmem_limit_bytes=VMEM_LIMIT, collective_id=0, has_side_effects=True
        ),
    )(*args)


def solution(mesh):
    placed = (
        P(("gx", "gy"), None, None, None),
        P(("gx", "gy"), None, None, None),
        P(("gx", "gy"), None),
        P(),
        P(),
        P(),
        P(),
    )
    return jax.shard_map(
        body,
        mesh=mesh,
        in_specs=placed,
        out_specs=P(("gx", "gy"), None, None, None),
        check_vma=False,
    )
```

time: 108 us -> 63.9 us (0.59)
  blocking collectives: 47.7 us -> 0 us
  Pallas kernels: 15.6 us -> 56.1 us
  starting transfers between devices: 18.7 us -> 0 us
  waiting for transfers between devices: 14 us -> 0 us
  local copies, waits for them, and re-layouts: 9.78 us -> 7.46 us
    all_to_all x2 -> x0, blocking collectives: 47.7 us -> none  [the longest x1 25.5 us: body(): got = lax.all_to_all(sums, 'gx', split_axis=0, concat_axis=0, tiled=True)]
    pallas_call x5 -> x1, Pallas kernels: 15.6 us -> 56.1 us  [body(): pl.pallas_call(functools.partial(fused, dims, groups, parts), out_shape=j...]
    all_to_all x2 -> x0, waiting for transfers between devices: 13.7 us -> none  [the longest x1 10.3 us: body(): back = lax.all_to_all(solved, 'gy', split_axis=0, concat_axis=0, tiled=True)]
    all_to_all x2 -> x0, starting transfers between devices: 11.3 us -> none  [the longest x1 7.49 us: body(): back = lax.all_to_all(solved, 'gy', split_axis=0, concat_axis=0, tiled=True)]
    ppermute x2 -> x0, starting transfers between devices: 7.38 us -> none  [the longest x1 4.37 us: body(): after = lax.ppermute(held[0], 'gx', down)]
    slice x1 -> x0, local copies, waits for them, and re-layouts: 1.44 us -> none  [type_rows(): real, imag = (wide[:, 0], wide[:, 1])]
    unnamed x17 -> x8, local copies, waits for them, and re-layouts: 4.64 us -> 5.24 us
  transfers between devices with their start and end apart: 4 -> 0, of which waited for: 3 -> 0; matrix products, arithmetic and copies ran while one was open for 2% -> 0% of each run, Pallas kernels for 0% -> 0%
where the time goes in v1:
time: 63.9 us; the launch traced here: 63.6 us
  Pallas kernels  56.1 us (88%)
  local copies, waits for them, and re-layouts  7.46 us (12%)
    pallas_call x1, Pallas kernels, body(): pl.pallas_call(functools.partial(fused, dims, groups, parts), out_shape=j...  56.1 us
    unnamed x8, local copies, waits for them, and re-layouts  5.24 us
    pallas_call x1, local copies, waits for them, and re-layouts, body(): pl.pallas_call(functools.partial(fused, dims, groups, parts), out_shape=j...  2.22 us

profile of v1, /device:TPU:1, one launch (start us, length us, event | category | flops | bytes accessed | tf_op | source)
XLA Modules:
  0.0 63.6 jit_solution(9237080586639235767)
XLA Ops:
  0.0 0.0 copy-start
  0.0 1.5 %copy.15.coupling = f32[2,24,20]{2,1,0:T(8,128)} copy(f32[2,24,20]{1,0,2:T(2,128)} %param.15) | data formatting | bytes 7680 | tf_op args[4]
  1.5 1.8 %copy.14.type_matrix = f32[16,2,20,20]{3,2,1,0:T(8,128)} copy(f32[16,2,20,20]{3,1,2,0:T(2,128)} %param.14) | data formatting | bytes 102400 | tf_op args[3]
  3.2 0.0 copy-done
  3.2 0.0 copy-start.1
  3.2 0.9 %copy.12.exciting = f32[2,2,20,1536]{3,2,1,0:T(8,128)} copy(f32[2,2,20,1536]{3,1,2,0:T(2,128)S(1)} %copy-done) | data formatting | bytes 983040 | tf_op args[0]
  4.1 0.2 copy-done.1
  4.3 0.9 %copy.13.incident = f32[2,2,20,1536]{3,2,1,0:T(8,128)} copy(f32[2,2,20,1536]{3,1,2,0:T(2,128)S(1)} %copy-done.1) | data formatting | bytes 983040 | tf_op args[1]
  5.2 56.1 %shard_map.109 = f32[2,2,20,1536]{3,2,1,0:T(8,128)} custom-call(f32[2,2,20,1536]{3,2,1,0:T(8,128)} %copy.12.exciting, f32[2,2,20,1536]{3,2,1,0:T(8,128)} %copy.13.incident, s32[2,1536]{1,0:T(2,128)} %kinds.1, f32[16,2,20,20]{3,2,1,0:T(8,128)} %copy.14.type_matrix, f32[2,24,20]{2,1,0:T(8,128)} %copy.15.coupling, f32[1,20]{1,0:T(1,128)} %bitcast.1, ...), custom_call_target="tpu_custom_call" | custom-call | tf_op jit(solution)/shard_map/pallas_call | solution.py:500
  61.4 2.2 %copy.16 = f32[2,2,20,1536]{3,1,2,0:T(2,128)} copy(f32[2,2,20,1536]{3,2,1,0:T(8,128)} %shard_map.109) | data formatting | bytes 983040 | tf_op jit(solution)/shard_map/pallas_call | solution.py:500
Async XLA Ops:
  0.0 3.2 %copy-start = (f32[2,2,20,1536]{3,1,2,0:T(2,128)S(1)}, f32[2,2,20,1536]{3,1,2,0:T(2,128)}, u32[]{:S(2)}) copy-start(f32[2,2,20,1536]{3,1,2,0:T(2,128)} %param.11) | copy-start | bytes 1474564
  3.2 1.1 %copy-start.1 = (f32[2,2,20,1536]{3,1,2,0:T(2,128)S(1)}, f32[2,2,20,1536]{3,1,2,0:T(2,128)}, u32[]{:S(2)}) copy-start(f32[2,2,20,1536]{3,1,2,0:T(2,128)} %param.12) | copy-start | bytes 1474564

commit v2 on v1

--- a/solution.py
+++ b/solution.py
@@ -106,7 +106,7 @@
     spread[...] = jnp.zeros_like(spread)
 
     def place(number, carry):
-        real, imag = type_matrix[number, 0], type_matrix[number, 1]
+        real, imag = type_matrix[number, :, 0, :], type_matrix[number, :, 1, :]
         for copy in range(3):
             low = 2 * GROUP * copy
             spread[number, 0:coef, low : low + coef] = real
@@ -129,8 +129,9 @@
     def add_chunk(col, carry):
         span = pl.ds(pl.multiple_of(col * chunk, chunk), chunk)
         empty = jnp.zeros((GROUP - coef, chunk), F32)
+
         joined = jnp.concatenate(
-            [exciting[row, 0, :, span], empty, exciting[row, 1, :, span], empty], axis=0
+            [exciting[row, :, 0, span], empty, exciting[row, :, 1, span], empty], axis=0
         )
         top = joined.astype(BF16)
         low = (joined - top.astype(F32)).astype(BF16)
@@ -177,10 +178,14 @@
             send[dest, row, part, used:slots, :] = blank
 
 
-def column_picker(gy, dims):
+def one_hot(gy, dims):
     rows, coef, width_x, used, slots, type_count = dims
     flat = gy * used + lax.broadcasted_iota(jnp.int32, (slots, coef), 0)
-    hit = flat % coef == lax.broadcasted_iota(jnp.int32, (slots, coef), 1)
+    return flat % coef == lax.broadcasted_iota(jnp.int32, (slots, coef), 1)
+
+
+def column_picker(gy, dims):
+    hit = one_hot(gy, dims)
 
     def pick(line):
         return jnp.sum(jnp.where(hit, line, 0.0), axis=1, keepdims=True)
@@ -203,31 +208,30 @@
     return loss
 
 
-def stage_backward(dims, got, incident, twiddle, matrix, out, work):
+def backward_row(row, dims, got, incident, twiddle, matrix, out, work):
     rows, coef, width_x, used, slots, type_count = dims
-    for row in range(rows):
+    for ka in range(OUTER):
+        for start, place, slot, count in pieces(ka, coef, used):
+            for part in range(2):
+                work[ka, start : start + count, part * LANES : (part + 1) * LANES] = got[
+                    place, row, part, slot : slot + count, :
+                ]
+        work[ka, coef:GROUP, :] = jnp.zeros((GROUP - coef, 2 * LANES), F32)
+    turned = dot32(work[...].reshape(OUTER * GROUP, 2 * LANES), matrix)
+    work[...] = turned.reshape(OUTER, GROUP, 2 * LANES)
+    for low in range(0, coef, 8):
+        count = min(8, coef - low)
+        values = []
         for ka in range(OUTER):
-            for start, place, slot, count in pieces(ka, coef, used):
-                for part in range(2):
-                    work[ka, start : start + count, part * LANES : (part + 1) * LANES] = got[
-                        place, row, part, slot : slot + count, :
-                    ]
-            work[ka, coef:GROUP, :] = jnp.zeros((GROUP - coef, 2 * LANES), F32)
-        turned = dot32(work[...].reshape(OUTER * GROUP, 2 * LANES), matrix)
-        work[...] = turned.reshape(OUTER, GROUP, 2 * LANES)
-        for low in range(0, coef, 8):
-            count = min(8, coef - low)
-            values = []
-            for ka in range(OUTER):
-                real = work[ka, low : low + count, 0:LANES]
-                imag = work[ka, low : low + count, LANES : 2 * LANES]
-                wr, wi = twiddle[ka, 0:1, :], twiddle[ka, 1:2, :]
-                values.append((real * wr + imag * wi, imag * wr - real * wi))
-            values = twelve_points(values, 1.0)
-            for a in range(OUTER):
-                for part in range(2):
-                    place = (row, part, slice(low, low + count), slice(a * LANES, (a + 1) * LANES))
-                    out[place] = incident[place] + values[a][part]
+            real = work[ka, low : low + count, 0:LANES]
+            imag = work[ka, low : low + count, LANES : 2 * LANES]
+            wr, wi = twiddle[ka, 0:1, :], twiddle[ka, 1:2, :]
+            values.append((real * wr + imag * wi, imag * wr - real * wi))
+        values = twelve_points(values, 1.0)
+        for a in range(OUTER):
+            for part in range(2):
+                place = (row, slice(low, low + count), part, slice(a * LANES, (a + 1) * LANES))
+                out[place] = incident[place] + values[a][part]
 
 
 def fused(
@@ -331,10 +335,14 @@
             reply.at[peer], ends.at[gx], reply_send.at[step], reply_recv.at[step], (peer, gy)
         )
 
-    def last(step):
+    def last(row, step):
         peer = near_peer(step)
         return remote(
-            solved.at[peer], back.at[gy], last_send.at[step], last_recv.at[step], (gx, peer)
+            solved.at[peer, row],
+            back.at[gy, row],
+            last_send.at[row, step],
+            last_recv.at[row, step],
+            (gx, peer),
         )
 
     up = remote(
@@ -366,14 +374,18 @@
     c1, s1 = phase[gy, 0], phase[gy, 1]
     c2, s2 = c1 * c1 - s1 * s1, 2.0 * c1 * s1
     turns = {-2: (c2, -s2), -1: (c1, -s1), 1: (c1, s1), 2: (c2, s2)}
+    chosen = [
+        jnp.dot(one_hot(gy, dims).astype(F32), coupling[:, p, :], precision=lax.Precision.HIGHEST)
+        * (1.0 / width_x)
+        for p in range(2)
+    ]
     number = 0
     for dy in range(-2, 3):
         real = imag = jnp.zeros((slots, LANES), F32)
         for dx in range(-2, 3):
             if dx == 0 and dy == 0:
                 continue
-            wr = pick(coupling[0, number : number + 1, :]) * (1.0 / width_x)
-            wi = pick(coupling[1, number : number + 1, :]) * (1.0 / width_x)
+            wr, wi = (chosen[p][:, number : number + 1] for p in range(2))
             number += 1
             if dx == 0:
                 real, imag = real + wr, imag + wi
@@ -438,30 +450,32 @@
             back_all[place, row, p] = behind[p]
         behind = tuple(behind[p] + held[1 + place, row, p] for p in range(2))
 
-    def combine(place, target):
+    def combine(row, place, target):
         gain_real, gain_imag = level[0], level[1]
-        for row in range(rows):
-            both = tuple(ahead_all[place, row, p] + back_all[place, row, p] for p in range(2))
-            real = gain_real * both[0] - gain_imag * both[1]
-            imag = gain_real * both[1] + gain_imag * both[0]
-            for dy in range(-2, 3):
-                jump, other = divmod(row + dy, rows)
-                wr, wi = near[dy + 2, 0], near[dy + 2, 1]
-                lr = held[1 + place + jump, other, 0]
-                li = held[1 + place + jump, other, 1]
-                real = real + (wr * lr - wi * li)
-                imag = imag + (wr * li + wi * lr)
-            target[place, row, 0] = real
-            target[place, row, 1] = imag
-
-    def solve(step):
-        combine(near_peer(step), solved)
-        last(step).start()
-
-    each(1, parts, solve)
-    combine(gy, back)
-    each(1, parts, lambda step: last(step).wait_recv())
-    stage_backward(dims, back, incident, twiddle, inverse, out, work)
+        both = tuple(ahead_all[place, row, p] + back_all[place, row, p] for p in range(2))
+        real = gain_real * both[0] - gain_imag * both[1]
+        imag = gain_real * both[1] + gain_imag * both[0]
+        for dy in range(-2, 3):
+            jump, other = divmod(row + dy, rows)
+            wr, wi = near[dy + 2, 0], near[dy + 2, 1]
+            lr = held[1 + place + jump, other, 0]
+            li = held[1 + place + jump, other, 1]
+            real = real + (wr * lr - wi * li)
+            imag = imag + (wr * li + wi * lr)
+        target[place, row, 0] = real
+        target[place, row, 1] = imag
+
+    for row in range(rows):
+
+        def solve(step, row=row):
+            combine(row, near_peer(step), solved)
+            last(row, step).start()
+
+        each(1, parts, solve)
+        combine(row, gy, back)
+    for row in range(rows):
+        each(1, parts, lambda step, row=row: last(row, step).wait_recv())
+        backward_row(row, dims, back, incident, twiddle, inverse, out, work)
 
     for row in range(rows):
         each(1, parts, lambda step, row=row: wide(row, step).wait_send())
@@ -469,7 +483,8 @@
     each(1, groups, lambda step: answer(step).wait_send())
     up.wait_send()
     down.wait_send()
-    each(1, parts, lambda step: last(step).wait_send())
+    for row in range(rows):
+        each(1, parts, lambda step, row=row: last(row, step).wait_send())
 
 
 def body(exciting, incident, pillar_type, type_matrix, near_coupling, screening, coupling_gain):
@@ -480,12 +495,14 @@
     slots = groups // 2
     dims = (rows, coef, width_x, used, slots, type_matrix.shape[0])
     twiddle, forward, inverse, phase = tables(width_x, coef, parts, slots, used)
+
+
     args = (
-        exciting,
-        incident,
+        exciting.transpose(0, 2, 1, 3),
+        incident.transpose(0, 2, 1, 3),
         pillar_type,
-        type_matrix,
-        near_coupling,
+        type_matrix.transpose(0, 2, 1, 3),
+        near_coupling.transpose(2, 0, 1),
         screening.reshape(1, coef),
         coupling_gain,
         twiddle,
@@ -497,9 +514,9 @@
     big = pltpu.VMEM((parts, rows, 2, slots, LANES), F32)
     small = pltpu.VMEM((groups, 2, LANES), F32)
     dma = pltpu.SemaphoreType.DMA
-    return pl.pallas_call(
+    result = pl.pallas_call(
         functools.partial(fused, dims, groups, parts),
-        out_shape=jax.ShapeDtypeStruct(exciting.shape, F32),
+        out_shape=jax.ShapeDtypeStruct((rows, coef, 2, width_x), F32),
         in_specs=[pl.BlockSpec(memory_space=pltpu.VMEM)] * len(args),
         out_specs=pl.BlockSpec(memory_space=pltpu.VMEM),
         scratch_shapes=[
@@ -528,13 +545,14 @@
             dma((groups,)),
             dma((2,)),
             dma((2,)),
-            dma((parts,)),
-            dma((parts,)),
+            dma((rows, parts)),
+            dma((rows, parts)),
         ],
         compiler_params=pltpu.CompilerParams(
             vmem_limit_bytes=VMEM_LIMIT, collective_id=0, has_side_effects=True
         ),
     )(*args)
+    return result.transpose(0, 2, 1, 3)
 
 
 def solution(mesh):

time: 63.9 us -> 58.6 us (0.917)
  local copies, waits for them, and re-layouts: 7.46 us -> 1.84 us
    unnamed x8 -> x1, local copies, waits for them, and re-layouts: 5.24 us -> 1.84 us
    pallas_call x1 -> x0, local copies, waits for them, and re-layouts: 2.22 us -> none  [body(): pl.pallas_call(functools.partial(fused, dims, groups, parts), out_shape=j...]
where the time goes in v2:
time: 58.6 us; the launch traced here: 58.4 us
  Pallas kernels  56.6 us (97%)
  local copies, waits for them, and re-layouts  1.84 us (3%)
    pallas_call x1, Pallas kernels, body(): pl.pallas_call(functools.partial(fused, dims, groups, parts), out_shape=j...  56.6 us
    unnamed x1, local copies, waits for them, and re-layouts  1.84 us

profile of v2, /device:TPU:1, one launch (start us, length us, event | category | flops | bytes accessed | tf_op | source)
XLA Modules:
  0.0 58.4 jit_solution(5937498450335917474)
XLA Ops:
  0.0 56.6 %shard_map.109 = f32[2,20,2,1536]{3,2,1,0:T(2,128)} custom-call(f32[2,20,2,1536]{3,2,1,0:T(2,128)} %bitcast.7, f32[2,20,2,1536]{3,2,1,0:T(2,128)} %bitcast.8, s32[2,1536]{1,0:T(2,128)} %kinds.1, f32[16,20,2,20]{3,2,1,0:T(2,128)} %bitcast.9, f32[20,2,24]{2,1,0:T(2,128)} %bitcast.10, f32[1,20]{1,0:T(1,128)} %bitcast.11, f32[2,20]{1,0:T(2,128)} %gain.1, ...), custom_call_target="tpu_custom_call" | custom-call | tf_op jit(solution)/shard_map/pallas_call | solution.py:517
  56.6 1.8 %copy.13 = f32[2,2,20,1536]{3,1,2,0:T(2,128)} copy(f32[2,2,20,1536]{3,1,2,0:T(2,128)} %bitcast.6) | data formatting | bytes 983040

commit v3 on v2

--- a/solution.py
+++ b/solution.py
@@ -15,6 +15,7 @@
 OUTER = 12
 LANES = 128
 GROUP = 24
+SUB = 8
 VMEM_LIMIT = 60 * 1024 * 1024
 
 
@@ -96,7 +97,7 @@
     start, found = 0, []
     while start < coef:
         part, slot = divmod(ka * coef + start, used)
-        count = min(coef - start, used - slot)
+        count = min(coef - start, used - slot, SUB - slot % SUB)
         found.append((start, part, slot, count))
         start += count
     return found
@@ -168,14 +169,14 @@
     for ka in range(OUTER):
         for start, dest, slot, count in pieces(ka, coef, used):
             for part in range(2):
-                send[dest, row, part, slot : slot + count, :] = turned[
+                send[dest, row, slot // SUB, part, slot % SUB : slot % SUB + count, :] = turned[
                     ka * GROUP + start : ka * GROUP + start + count,
                     part * LANES : (part + 1) * LANES,
                 ]
     blank = jnp.zeros((slots - used, LANES), F32)
     for dest in range(send.shape[0]):
         for part in range(2):
-            send[dest, row, part, used:slots, :] = blank
+            send[dest, row, used // SUB, part, used % SUB : SUB, :] = blank
 
 
 def one_hot(gy, dims):
@@ -214,7 +215,7 @@
         for start, place, slot, count in pieces(ka, coef, used):
             for part in range(2):
                 work[ka, start : start + count, part * LANES : (part + 1) * LANES] = got[
-                    place, row, part, slot : slot + count, :
+                    place, row, slot // SUB, part, slot % SUB : slot % SUB + count, :
                 ]
         work[ka, coef:GROUP, :] = jnp.zeros((GROUP - coef, 2 * LANES), F32)
     turned = dot32(work[...].reshape(OUTER * GROUP, 2 * LANES), matrix)
@@ -281,6 +282,7 @@
     rows, coef, width_x, used, slots, type_count = dims
     gx, gy = lax.axis_index("gx"), lax.axis_index("gy")
     length = parts * rows
+    halves = range(slots // SUB)
 
     def near_peer(step):
         return lax.rem(gy + step, parts)
@@ -313,35 +315,43 @@
     each(1, parts, lambda step: greet((gx, near_peer(step))))
     each(1, groups, lambda step: greet((far_peer(step), gy)))
 
-    def wide(row, step):
+    def wide(row, half, step):
         peer = near_peer(step)
         return remote(
-            send.at[peer, row],
-            held.at[1 + gy, row],
-            wide_send.at[row, step],
-            wide_recv.at[row, step],
+            send.at[peer, row, half],
+            held.at[1 + gy, row, half],
+            wide_send.at[row, half, step],
+            wide_recv.at[row, half, step],
             (gx, peer),
         )
 
-    def small(step):
+    def small(half, step):
         peer = far_peer(step)
         return remote(
-            sums.at[peer], got.at[gx], small_send.at[step], small_recv.at[step], (peer, gy)
-        )
-
-    def answer(step):
+            sums.at[half, peer],
+            got.at[half, gx],
+            small_send.at[half, step],
+            small_recv.at[half, step],
+            (peer, gy),
+        )
+
+    def answer(half, step):
         peer = far_peer(step)
         return remote(
-            reply.at[peer], ends.at[gx], reply_send.at[step], reply_recv.at[step], (peer, gy)
-        )
-
-    def last(row, step):
+            reply.at[half, peer],
+            ends.at[half, gx],
+            reply_send.at[half, step],
+            reply_recv.at[half, step],
+            (peer, gy),
+        )
+
+    def last(row, half, step):
         peer = near_peer(step)
         return remote(
-            solved.at[peer, row],
-            back.at[gy, row],
-            last_send.at[row, step],
-            last_recv.at[row, step],
+            solved.at[peer, row, half],
+            back.at[gy, row, half],
+            last_send.at[row, half, step],
+            last_recv.at[row, half, step],
             (gx, peer),
         )
 
@@ -361,7 +371,8 @@
         forward_row(row, dims, exciting, kinds, twiddle, forward, send, stacked, field, work)
         if row == 0:
             pl.semaphore_wait(barrier, parts + groups - 2)
-        each(1, parts, lambda step, row=row: wide(row, step).start())
+        for half in halves:
+            each(1, parts, lambda step, row=row, half=half: wide(row, half, step).start())
         held[1 + gy, row] = send[gy, row]
 
     pick, screen, width, loss = decay(gy, dims, phase, screening)
@@ -395,96 +406,103 @@
         near[dy + 2, 0] = real
         near[dy + 2, 1] = imag
 
-    for row in range(rows):
-        each(1, parts, lambda step, row=row: wide(row, step).wait_recv())
-    up.start()
-    down.start()
-    ratio = level[3]
-    zero = jnp.zeros((slots, LANES), F32)
-    ahead, behind = (zero, zero), (zero, zero)
-    for step in range(length):
-        place, row = divmod(step, rows)
-        ahead = tuple(ratio * ahead[p] + held[1 + place, row, p] for p in range(2))
-        place, row = divmod(length - 1 - step, rows)
-        behind = tuple(ratio * behind[p] + held[1 + place, row, p] for p in range(2))
-    for slot in range(slots):
-        for part in range(2):
-            sums[2 * slot, part : part + 1, :] = ahead[part][slot : slot + 1]
-            sums[2 * slot + 1, part : part + 1, :] = behind[part][slot : slot + 1]
-    each(1, groups, lambda step: small(step).start())
-    got[gx] = sums[gx]
-
-    loss = level[2, pl.ds(gx // 2, 1), :]
-    side = gx % 2
-    ratio = 1.0 - loss
-    whole = repeated(loss, groups)
-    each(1, groups, lambda step: small(step).wait_recv())
-    total = jnp.zeros((2, LANES), F32)
-    for step in range(groups):
-        total = ratio * total + got[step + side * (groups - 1 - 2 * step)]
-    total = total / whole
-    for step in range(groups):
-        place = step + side * (groups - 1 - 2 * step)
-        reply[place] = total
-        total = ratio * total + got[place]
-    each(1, groups, lambda step: answer(step).start())
-    ends[gx] = reply[gx]
-    each(1, groups, lambda step: answer(step).wait_recv())
+    zero = jnp.zeros((SUB, LANES), F32)
+    for half in halves:
+        for row in range(rows):
+            each(1, parts, lambda step, row=row, half=half: wide(row, half, step).wait_recv())
+        if half == halves[-1]:
+            up.start()
+            down.start()
+        ratio = level[3, SUB * half : SUB * (half + 1), :]
+        ahead, behind = (zero, zero), (zero, zero)
+        for step in range(length):
+            place, row = divmod(step, rows)
+            ahead = tuple(ratio * ahead[p] + held[1 + place, row, half, p] for p in range(2))
+            place, row = divmod(length - 1 - step, rows)
+            behind = tuple(ratio * behind[p] + held[1 + place, row, half, p] for p in range(2))
+        for slot in range(SUB):
+            for part in range(2):
+                sums[half, 4 * slot + part] = ahead[part][slot : slot + 1]
+                sums[half, 4 * slot + 2 + part] = behind[part][slot : slot + 1]
+        each(1, groups, lambda step, half=half: small(half, step).start())
+        got[half, gx] = sums[half, gx]
+
+    side = gx // 2 % 2
+    for half in halves:
+        loss = level[2, pl.ds(SUB * half + gx // 4, 1), :]
+        ratio = 1.0 - loss
+        whole = repeated(loss, groups)
+        each(1, groups, lambda step, half=half: small(half, step).wait_recv())
+        total = jnp.zeros((1, LANES), F32)
+        for step in range(groups):
+            total = ratio * total + got[half, step + side * (groups - 1 - 2 * step)]
+        total = total / whole
+        for step in range(groups):
+            place = step + side * (groups - 1 - 2 * step)
+            reply[half, place] = total
+            total = ratio * total + got[half, place]
+        each(1, groups, lambda step, half=half: answer(half, step).start())
+        ends[half, gx] = reply[half, gx]
+
     up.wait_recv()
     down.wait_recv()
 
-    for slot in range(slots):
-        for part in range(2):
-            edge[0, part, slot : slot + 1, :] = ends[2 * slot, part : part + 1, :]
-            edge[1, part, slot : slot + 1, :] = ends[2 * slot + 1, part : part + 1, :]
-    ratio = level[3]
-    ahead, behind = (edge[0, 0], edge[0, 1]), (edge[1, 0], edge[1, 1])
-    for step in range(length):
-        place, row = divmod(step, rows)
-        ahead = tuple(ratio * ahead[p] + held[1 + place, row, p] for p in range(2))
-        for p in range(2):
-            ahead_all[place, row, p] = ahead[p]
-        place, row = divmod(length - 1 - step, rows)
-        behind = tuple(ratio * behind[p] for p in range(2))
-        for p in range(2):
-            back_all[place, row, p] = behind[p]
-        behind = tuple(behind[p] + held[1 + place, row, p] for p in range(2))
-
-    def combine(row, place, target):
-        gain_real, gain_imag = level[0], level[1]
+    def combine(row, half, place, target):
+        span = slice(SUB * half, SUB * (half + 1))
+        gain_real, gain_imag = level[0, span, :], level[1, span, :]
         both = tuple(ahead_all[place, row, p] + back_all[place, row, p] for p in range(2))
         real = gain_real * both[0] - gain_imag * both[1]
         imag = gain_real * both[1] + gain_imag * both[0]
         for dy in range(-2, 3):
             jump, other = divmod(row + dy, rows)
-            wr, wi = near[dy + 2, 0], near[dy + 2, 1]
-            lr = held[1 + place + jump, other, 0]
-            li = held[1 + place + jump, other, 1]
+            wr, wi = near[dy + 2, 0, span, :], near[dy + 2, 1, span, :]
+            lr = held[1 + place + jump, other, half, 0]
+            li = held[1 + place + jump, other, half, 1]
             real = real + (wr * lr - wi * li)
             imag = imag + (wr * li + wi * lr)
-        target[place, row, 0] = real
-        target[place, row, 1] = imag
+        target[place, row, half, 0] = real
+        target[place, row, half, 1] = imag
+
+    for half in halves:
+        each(1, groups, lambda step, half=half: answer(half, step).wait_recv())
+        for slot in range(SUB):
+            for part in range(2):
+                for way in range(2):
+                    edge[way, part, slot : slot + 1, :] = ends[half, 4 * slot + 2 * way + part]
+        ratio = level[3, SUB * half : SUB * (half + 1), :]
+        ahead, behind = (edge[0, 0], edge[0, 1]), (edge[1, 0], edge[1, 1])
+        for step in range(length):
+            place, row = divmod(step, rows)
+            ahead = tuple(ratio * ahead[p] + held[1 + place, row, half, p] for p in range(2))
+            for p in range(2):
+                ahead_all[place, row, p] = ahead[p]
+            place, row = divmod(length - 1 - step, rows)
+            behind = tuple(ratio * behind[p] for p in range(2))
+            for p in range(2):
+                back_all[place, row, p] = behind[p]
+            behind = tuple(behind[p] + held[1 + place, row, half, p] for p in range(2))
+        for row in range(rows):
+
+            def solve(step, row=row, half=half):
+                combine(row, half, near_peer(step), solved)
+                last(row, half, step).start()
+
+            each(1, parts, solve)
+            combine(row, half, gy, back)
 
     for row in range(rows):
-
-        def solve(step, row=row):
-            combine(row, near_peer(step), solved)
-            last(row, step).start()
-
-        each(1, parts, solve)
-        combine(row, gy, back)
-    for row in range(rows):
-        each(1, parts, lambda step, row=row: last(row, step).wait_recv())
+        for half in halves:
+            each(1, parts, lambda step, row=row, half=half: last(row, half, step).wait_recv())
         backward_row(row, dims, back, incident, twiddle, inverse, out, work)
 
-    for row in range(rows):
-        each(1, parts, lambda step, row=row: wide(row, step).wait_send())
-    each(1, groups, lambda step: small(step).wait_send())
-    each(1, groups, lambda step: answer(step).wait_send())
     up.wait_send()
     down.wait_send()
-    for row in range(rows):
-        each(1, parts, lambda step, row=row: last(row, step).wait_send())
+    for half in halves:
+        for row in range(rows):
+            each(1, parts, lambda step, row=row, half=half: wide(row, half, step).wait_send())
+            each(1, parts, lambda step, row=row, half=half: last(row, half, step).wait_send())
+        each(1, groups, lambda step, half=half: small(half, step).wait_send())
+        each(1, groups, lambda step, half=half: answer(half, step).wait_send())
 
 
 def body(exciting, incident, pillar_type, type_matrix, near_coupling, screening, coupling_gain):
@@ -511,8 +529,10 @@
         phase,
     )
     count = type_matrix.shape[0]
-    big = pltpu.VMEM((parts, rows, 2, slots, LANES), F32)
-    small = pltpu.VMEM((groups, 2, LANES), F32)
+    halves = slots // SUB
+    big = pltpu.VMEM((parts, rows, halves, 2, SUB, LANES), F32)
+    line = pltpu.VMEM((parts, rows, 2, SUB, LANES), F32)
+    small = pltpu.VMEM((halves, groups, 1, LANES), F32)
     dma = pltpu.SemaphoreType.DMA
     result = pl.pallas_call(
         functools.partial(fused, dims, groups, parts),
@@ -525,28 +545,28 @@
             pltpu.VMEM((OUTER, 2, GROUP, LANES), F32),
             pltpu.VMEM((OUTER, GROUP, 2 * LANES), F32),
             big,
-            pltpu.VMEM((parts + 2, rows, 2, slots, LANES), F32),
+            pltpu.VMEM((parts + 2, rows, halves, 2, SUB, LANES), F32),
             small,
             small,
             small,
             small,
-            pltpu.VMEM((2, 2, slots, LANES), F32),
+            pltpu.VMEM((2, 2, SUB, LANES), F32),
             pltpu.VMEM((5, 2, slots, LANES), F32),
             pltpu.VMEM((4, slots, LANES), F32),
+            line,
+            line,
             big,
             big,
-            big,
-            big,
-            dma((rows, parts)),
-            dma((rows, parts)),
-            dma((groups,)),
-            dma((groups,)),
-            dma((groups,)),
-            dma((groups,)),
+            dma((rows, halves, parts)),
+            dma((rows, halves, parts)),
+            dma((halves, groups)),
+            dma((halves, groups)),
+            dma((halves, groups)),
+            dma((halves, groups)),
             dma((2,)),
             dma((2,)),
-            dma((rows, parts)),
-            dma((rows, parts)),
+            dma((rows, halves, parts)),
+            dma((rows, halves, parts)),
         ],
         compiler_params=pltpu.CompilerParams(
             vmem_limit_bytes=VMEM_LIMIT, collective_id=0, has_side_effects=True

time: 58.6 us -> 60.9 us (1.039)
  Pallas kernels: 56.6 us -> 58.9 us
    pallas_call x1, Pallas kernels: 56.6 us -> 58.9 us  [body(): pl.pallas_call(functools.partial(fused, dims, groups, parts), out_shape=j...]
where the time goes in v3:
time: 60.9 us; the launch traced here: 60.7 us
  Pallas kernels  58.9 us (97%)
  local copies, waits for them, and re-layouts  1.84 us (3%)
    pallas_call x1, Pallas kernels, body(): pl.pallas_call(functools.partial(fused, dims, groups, parts), out_shape=j...  58.9 us
    unnamed x1, local copies, waits for them, and re-layouts  1.84 us

profile of v3, /device:TPU:1, one launch (start us, length us, event | category | flops | bytes accessed | tf_op | source)
XLA Modules:
  0.0 60.7 jit_solution(18332890733054040307)
XLA Ops:
  0.0 58.9 %shard_map.109 = f32[2,20,2,1536]{3,2,1,0:T(2,128)} custom-call(f32[2,20,2,1536]{3,2,1,0:T(2,128)} %bitcast.7, f32[2,20,2,1536]{3,2,1,0:T(2,128)} %bitcast.8, s32[2,1536]{1,0:T(2,128)} %kinds.1, f32[16,20,2,20]{3,2,1,0:T(2,128)} %bitcast.9, f32[20,2,24]{2,1,0:T(2,128)} %bitcast.10, f32[1,20]{1,0:T(1,128)} %bitcast.11, f32[2,20]{1,0:T(2,128)} %gain.1, ...), custom_call_target="tpu_custom_call" | custom-call | tf_op jit(solution)/shard_map/pallas_call | solution.py:537
  58.9 1.8 %copy.13 = f32[2,2,20,1536]{3,1,2,0:T(2,128)} copy(f32[2,2,20,1536]{3,1,2,0:T(2,128)} %bitcast.6) | data formatting | bytes 983040

commit v4 on v2

--- a/solution.py
+++ b/solution.py
@@ -305,6 +305,10 @@
 
         lax.fori_loop(low, high, run, 0)
 
+    def settle(ref, sem):
+        pltpu.make_async_copy(ref, ref, sem).wait()
+
+    others, rest = pl.ds(0, parts - 1), pl.ds(0, groups - 1)
     barrier = pltpu.get_barrier_semaphore()
 
     def greet(device):
@@ -318,21 +322,21 @@
         return remote(
             send.at[peer, row],
             held.at[1 + gy, row],
-            wide_send.at[row, step],
-            wide_recv.at[row, step],
+            wide_send.at[row],
+            wide_recv.at[row],
             (gx, peer),
         )
 
     def small(step):
         peer = far_peer(step)
         return remote(
-            sums.at[peer], got.at[gx], small_send.at[step], small_recv.at[step], (peer, gy)
+            sums.at[peer], got.at[gx], small_send.at[0], small_recv.at[0], (peer, gy)
         )
 
     def answer(step):
         peer = far_peer(step)
         return remote(
-            reply.at[peer], ends.at[gx], reply_send.at[step], reply_recv.at[step], (peer, gy)
+            reply.at[peer], ends.at[gx], reply_send.at[0], reply_recv.at[0], (peer, gy)
         )
 
     def last(row, step):
@@ -340,8 +344,8 @@
         return remote(
             solved.at[peer, row],
             back.at[gy, row],
-            last_send.at[row, step],
-            last_recv.at[row, step],
+            last_send.at[row],
+            last_recv.at[row],
             (gx, peer),
         )
 
@@ -396,7 +400,7 @@
         near[dy + 2, 1] = imag
 
     for row in range(rows):
-        each(1, parts, lambda step, row=row: wide(row, step).wait_recv())
+        settle(held.at[others, row], wide_recv.at[row])
     up.start()
     down.start()
     ratio = level[3]
@@ -418,7 +422,7 @@
     side = gx % 2
     ratio = 1.0 - loss
     whole = repeated(loss, groups)
-    each(1, groups, lambda step: small(step).wait_recv())
+    settle(got.at[rest], small_recv.at[0])
     total = jnp.zeros((2, LANES), F32)
     for step in range(groups):
         total = ratio * total + got[step + side * (groups - 1 - 2 * step)]
@@ -429,7 +433,7 @@
         total = ratio * total + got[place]
     each(1, groups, lambda step: answer(step).start())
     ends[gx] = reply[gx]
-    each(1, groups, lambda step: answer(step).wait_recv())
+    settle(ends.at[rest], reply_recv.at[0])
     up.wait_recv()
     down.wait_recv()
 
@@ -474,17 +478,17 @@
         each(1, parts, solve)
         combine(row, gy, back)
     for row in range(rows):
-        each(1, parts, lambda step, row=row: last(row, step).wait_recv())
+        settle(back.at[others, row], last_recv.at[row])
         backward_row(row, dims, back, incident, twiddle, inverse, out, work)
 
     for row in range(rows):
-        each(1, parts, lambda step, row=row: wide(row, step).wait_send())
-    each(1, groups, lambda step: small(step).wait_send())
-    each(1, groups, lambda step: answer(step).wait_send())
+        settle(send.at[others, row], wide_send.at[row])
+    settle(sums.at[rest], small_send.at[0])
+    settle(reply.at[rest], reply_send.at[0])
     up.wait_send()
     down.wait_send()
     for row in range(rows):
-        each(1, parts, lambda step, row=row: last(row, step).wait_send())
+        settle(solved.at[others, row], last_send.at[row])
 
 
 def body(exciting, incident, pillar_type, type_matrix, near_coupling, screening, coupling_gain):
@@ -537,16 +541,16 @@
             big,
             big,
             big,
-            dma((rows, parts)),
-            dma((rows, parts)),
-            dma((groups,)),
-            dma((groups,)),
-            dma((groups,)),
-            dma((groups,)),
+            dma((rows,)),
+            dma((rows,)),
+            dma((1,)),
+            dma((1,)),
+            dma((1,)),
+            dma((1,)),
             dma((2,)),
             dma((2,)),
-            dma((rows, parts)),
-            dma((rows, parts)),
+            dma((rows,)),
+            dma((rows,)),
         ],
         compiler_params=pltpu.CompilerParams(
             vmem_limit_bytes=VMEM_LIMIT, collective_id=0, has_side_effects=True

time: 58.6 us -> 55.5 us (0.947)
  Pallas kernels: 56.6 us -> 53.4 us
    pallas_call x1, Pallas kernels: 56.6 us -> 53.4 us  [body(): pl.pallas_call(functools.partial(fused, dims, groups, parts), out_shape=j...]
where the time goes in v4:
time: 55.5 us; the launch traced here: 55.3 us
  Pallas kernels  53.4 us (96%)
  local copies, waits for them, and re-layouts  1.84 us (3%)
    pallas_call x1, Pallas kernels, body(): pl.pallas_call(functools.partial(fused, dims, groups, parts), out_shape=j...  53.4 us
    unnamed x1, local copies, waits for them, and re-layouts  1.84 us

profile of v4, /device:TPU:1, one launch (start us, length us, event | category | flops | bytes accessed | tf_op | source)
XLA Modules:
  0.0 55.3 jit_solution(14101643384532111361)
XLA Ops:
  0.0 53.4 %shard_map.109 = f32[2,20,2,1536]{3,2,1,0:T(2,128)} custom-call(f32[2,20,2,1536]{3,2,1,0:T(2,128)} %bitcast.7, f32[2,20,2,1536]{3,2,1,0:T(2,128)} %bitcast.8, s32[2,1536]{1,0:T(2,128)} %kinds.1, f32[16,20,2,20]{3,2,1,0:T(2,128)} %bitcast.9, f32[20,2,24]{2,1,0:T(2,128)} %bitcast.10, f32[1,20]{1,0:T(1,128)} %bitcast.11, f32[2,20]{1,0:T(2,128)} %gain.1, ...), custom_call_target="tpu_custom_call" | custom-call | tf_op jit(solution)/shard_map/pallas_call | solution.py:521
  53.5 1.8 %copy.13 = f32[2,2,20,1536]{3,1,2,0:T(2,128)} copy(f32[2,2,20,1536]{3,1,2,0:T(2,128)} %bitcast.6) | data formatting | bytes 983040

commit v5 on v4

--- a/solution.py
+++ b/solution.py
@@ -299,11 +299,18 @@
         )
 
     def each(low, high, act):
-        def run(step, carry):
+        for step in range(low, high):
             act(step)
+
+    def looped(low, high, act):
+        stride = 3 if (high - low) % 3 == 0 else 1
+
+        def run(index, carry):
+            for offset in range(stride):
+                act(low + index * stride + offset)
             return carry
 
-        lax.fori_loop(low, high, run, 0)
+        lax.fori_loop(0, (high - low) // stride, run, 0)
 
     def settle(ref, sem):
         pltpu.make_async_copy(ref, ref, sem).wait()
@@ -475,7 +482,7 @@
             combine(row, near_peer(step), solved)
             last(row, step).start()
 
-        each(1, parts, solve)
+        looped(1, parts, solve)
         combine(row, gy, back)
     for row in range(rows):
         settle(back.at[others, row], last_recv.at[row])

time: 55.5 us -> 55.2 us (level)
  no operation moved by 1% of the time
where the time goes in v5:
time: 55.2 us; the launch traced here: 55 us
  Pallas kernels  53.2 us (96%)
  local copies, waits for them, and re-layouts  1.84 us (3%)
    pallas_call x1, Pallas kernels, body(): pl.pallas_call(functools.partial(fused, dims, groups, parts), out_shape=j...  53.2 us
    unnamed x1, local copies, waits for them, and re-layouts  1.84 us

profile of v5, /device:TPU:1, one launch (start us, length us, event | category | flops | bytes accessed | tf_op | source)
XLA Modules:
  0.0 55.0 jit_solution(2285773720955181032)
XLA Ops:
  0.0 53.2 %shard_map.109 = f32[2,20,2,1536]{3,2,1,0:T(2,128)} custom-call(f32[2,20,2,1536]{3,2,1,0:T(2,128)} %bitcast.7, f32[2,20,2,1536]{3,2,1,0:T(2,128)} %bitcast.8, s32[2,1536]{1,0:T(2,128)} %kinds.1, f32[16,20,2,20]{3,2,1,0:T(2,128)} %bitcast.9, f32[20,2,24]{2,1,0:T(2,128)} %bitcast.10, f32[1,20]{1,0:T(1,128)} %bitcast.11, f32[2,20]{1,0:T(2,128)} %gain.1, ...), custom_call_target="tpu_custom_call" | custom-call | tf_op jit(solution)/shard_map/pallas_call | solution.py:528
  53.2 1.8 %copy.13 = f32[2,2,20,1536]{3,1,2,0:T(2,128)} copy(f32[2,2,20,1536]{3,1,2,0:T(2,128)} %bitcast.6) | data formatting | bytes 983040

commit v6 on v3

--- a/solution.py
+++ b/solution.py
@@ -307,6 +307,10 @@
 
         lax.fori_loop(low, high, run, 0)
 
+    def settle(ref, sem):
+        pltpu.make_async_copy(ref, ref, sem).wait()
+
+    others, rest = pl.ds(0, parts - 1), pl.ds(0, groups - 1)
     barrier = pltpu.get_barrier_semaphore()
 
     def greet(device):
@@ -320,8 +324,8 @@
         return remote(
             send.at[peer, row, half],
             held.at[1 + gy, row, half],
-            wide_send.at[row, half, step],
-            wide_recv.at[row, half, step],
+            wide_send.at[row, half],
+            wide_recv.at[row, half],
             (gx, peer),
         )
 
@@ -330,8 +334,8 @@
         return remote(
             sums.at[half, peer],
             got.at[half, gx],
-            small_send.at[half, step],
-            small_recv.at[half, step],
+            small_send.at[half],
+            small_recv.at[half],
             (peer, gy),
         )
 
@@ -340,8 +344,8 @@
         return remote(
             reply.at[half, peer],
             ends.at[half, gx],
-            reply_send.at[half, step],
-            reply_recv.at[half, step],
+            reply_send.at[half],
+            reply_recv.at[half],
             (peer, gy),
         )
 
@@ -350,8 +354,8 @@
         return remote(
             solved.at[peer, row, half],
             back.at[gy, row, half],
-            last_send.at[row, half, step],
-            last_recv.at[row, half, step],
+            last_send.at[row, half],
+            last_recv.at[row, half],
             (gx, peer),
         )
 
@@ -409,7 +413,7 @@
     zero = jnp.zeros((SUB, LANES), F32)
     for half in halves:
         for row in range(rows):
-            each(1, parts, lambda step, row=row, half=half: wide(row, half, step).wait_recv())
+            settle(held.at[others, row, half], wide_recv.at[row, half])
         if half == halves[-1]:
             up.start()
             down.start()
@@ -432,7 +436,7 @@
         loss = level[2, pl.ds(SUB * half + gx // 4, 1), :]
         ratio = 1.0 - loss
         whole = repeated(loss, groups)
-        each(1, groups, lambda step, half=half: small(half, step).wait_recv())
+        settle(got.at[half, rest], small_recv.at[half])
         total = jnp.zeros((1, LANES), F32)
         for step in range(groups):
             total = ratio * total + got[half, step + side * (groups - 1 - 2 * step)]
@@ -464,7 +468,7 @@
         target[place, row, half, 1] = imag
 
     for half in halves:
-        each(1, groups, lambda step, half=half: answer(half, step).wait_recv())
+        settle(ends.at[half, rest], reply_recv.at[half])
         for slot in range(SUB):
             for part in range(2):
                 for way in range(2):
@@ -492,17 +496,17 @@
 
     for row in range(rows):
         for half in halves:
-            each(1, parts, lambda step, row=row, half=half: last(row, half, step).wait_recv())
+            settle(back.at[others, row, half], last_recv.at[row, half])
         backward_row(row, dims, back, incident, twiddle, inverse, out, work)
 
     up.wait_send()
     down.wait_send()
     for half in halves:
         for row in range(rows):
-            each(1, parts, lambda step, row=row, half=half: wide(row, half, step).wait_send())
-            each(1, parts, lambda step, row=row, half=half: last(row, half, step).wait_send())
-        each(1, groups, lambda step, half=half: small(half, step).wait_send())
-        each(1, groups, lambda step, half=half: answer(half, step).wait_send())
+            settle(send.at[others, row, half], wide_send.at[row, half])
+            settle(solved.at[others, row, half], last_send.at[row, half])
+        settle(sums.at[half, rest], small_send.at[half])
+        settle(reply.at[half, rest], reply_send.at[half])
 
 
 def body(exciting, incident, pillar_type, type_matrix, near_coupling, screening, coupling_gain):
@@ -557,16 +561,16 @@
             line,
             big,
             big,
-            dma((rows, halves, parts)),
-            dma((rows, halves, parts)),
-            dma((halves, groups)),
-            dma((halves, groups)),
-            dma((halves, groups)),
-            dma((halves, groups)),
+            dma((rows, halves)),
+            dma((rows, halves)),
+            dma((halves,)),
+            dma((halves,)),
+            dma((halves,)),
+            dma((halves,)),
             dma((2,)),
             dma((2,)),
-            dma((rows, halves, parts)),
-            dma((rows, halves, parts)),
+            dma((rows, halves)),
+            dma((rows, halves)),
         ],
         compiler_params=pltpu.CompilerParams(
             vmem_limit_bytes=VMEM_LIMIT, collective_id=0, has_side_effects=True

time: 60.9 us -> 54.6 us (0.90)
  Pallas kernels: 58.9 us -> 52.6 us
    pallas_call x1, Pallas kernels: 58.9 us -> 52.6 us  [body(): pl.pallas_call(functools.partial(fused, dims, groups, parts), out_shape=j...]
where the time goes in v6:
time: 54.6 us; the launch traced here: 54.4 us
  Pallas kernels  52.6 us (96%)
  local copies, waits for them, and re-layouts  1.84 us (3%)
    pallas_call x1, Pallas kernels, body(): pl.pallas_call(functools.partial(fused, dims, groups, parts), out_shape=j...  52.6 us
    unnamed x1, local copies, waits for them, and re-layouts  1.84 us

profile of v6, /device:TPU:1, one launch (start us, length us, event | category | flops | bytes accessed | tf_op | source)
XLA Modules:
  0.0 54.4 jit_solution(1974325561276809570)
XLA Ops:
  0.0 52.6 %shard_map.109 = f32[2,20,2,1536]{3,2,1,0:T(2,128)} custom-call(f32[2,20,2,1536]{3,2,1,0:T(2,128)} %bitcast.7, f32[2,20,2,1536]{3,2,1,0:T(2,128)} %bitcast.8, s32[2,1536]{1,0:T(2,128)} %kinds.1, f32[16,20,2,20]{3,2,1,0:T(2,128)} %bitcast.9, f32[20,2,24]{2,1,0:T(2,128)} %bitcast.10, f32[1,20]{1,0:T(1,128)} %bitcast.11, f32[2,20]{1,0:T(2,128)} %gain.1, ...), custom_call_target="tpu_custom_call" | custom-call | tf_op jit(solution)/shard_map/pallas_call | solution.py:541
  52.6 1.8 %copy.13 = f32[2,2,20,1536]{3,1,2,0:T(2,128)} copy(f32[2,2,20,1536]{3,1,2,0:T(2,128)} %bitcast.6) | data formatting | bytes 983040
